TPU v7x, 256 devices: a whole 4x4x8 slice. The times are simulated.
256 devices in a mesh: gx: 16 (over z, x_hi), gy: 16 (over y, x_lo, core).
Axes of the slice: x: 4 (x_hi: 2, x_lo: 2; x = x_hi * 2 + x_lo), y: 4, z: 8, core: 2. Of those that a mesh axis runs over, the one named last changes fastest.
Arguments:
- map_codes: int32 [4096, 4096], P('gy', 'gx'), may hold values from 0 to 63
- reward_table: float32 [4, 64], replicated, may hold values from -1 to 1
- start_cell: int32 [524288], P(('gx', 'gy')), may hold values from 0 to 65535, as said below
- agent_task: int32 [524288], P(('gx', 'gy')), may hold values from 0 to 3
- actions: int32 [16, 524288], P(None, ('gx', 'gy')), may hold values from 0 to 4, as said below
Outputs:
- values: float32 [4, 4096, 4096], P(None, 'gy', 'gx')
- agent_value: float32 [524288], P(('gx', 'gy'))
Inputs may be any that keep to these rules, and one draw needn't show every extreme that they name: `start_cell`: each agent starts inside the tile of its block. `actions`: 0 stays, 1 and 2 move one row up and down, 3 and 4 one column left and right. After its moves every agent stands in its starting tile or in one of the eight tiles around it (diagonal ones included); at most 128 agents of one block stand in any one of those eight tiles, and for every block exactly 128 stand in one of them.
All inputs are finite; a program needn't handle non-finite values.
Results may differ from a plain program's by a relative error of at most 0.00026.
Values sent between devices are 32-bit elements; how exact they have to be, the bound alone decides.
A program may use at most 64 MiB of HBM per device.

v0:
```python
import math

import jax
import jax.numpy as jnp
from jax import lax
from jax.sharding import PartitionSpec as P

CAP = 128
SWEEPS = 16
CODES = 64
TERMINAL = 2


GAMMA = 0.95
PENALTY = 0.5
NEIGHBOURS = ((-1, -1), (-1, 0), (-1, 1), (0, -1), (0, 1), (1, -1), (1, 0), (1, 1))


def from_behind(value, axis, steps):
    count = lax.axis_size(axis)
    pairs = [(source, (source + steps) % count) for source in range(count)]
    return lax.ppermute(value, axis, pairs)


def with_halo(block, sides, width):
    for axis, dim in sides:
        count = lax.axis_size(axis)
        forward = [(i, i + 1) for i in range(count - 1)]
        forward.append((count - 1, 0))
        backward = [(target, source) for source, target in forward]
        low = lax.ppermute(
            lax.slice_in_dim(block, block.shape[dim] - width, None, axis=dim), axis, forward
        )
        high = lax.ppermute(lax.slice_in_dim(block, 0, width, axis=dim), axis, backward)
        block = jnp.concatenate([low, block, high], axis=dim)
    return block


def sweep_cells(reward, living, padded):
    from_above = padded[..., :-2, 1:-1]
    from_below = padded[..., 2:, 1:-1]
    from_left = padded[..., 1:-1, :-2]
    from_right = padded[..., 1:-1, 2:]
    highest = jnp.maximum(jnp.maximum(from_above, from_below), jnp.maximum(from_left, from_right))
    return reward + GAMMA * living * highest


def margin_part(padded, margin):
    offset = 4 - margin
    return padded[..., offset : padded.shape[-2] - offset, offset : padded.shape[-1] - offset]


def deliver(parcels):
    arrived = {}
    passed = {}
    for col_step in (-1, 1):
        bundle = jnp.stack([parcels[-1, col_step], parcels[0, col_step], parcels[1, col_step]])
        bundle = from_behind(bundle, "gx", col_step)
        passed[-1, col_step] = bundle[0]
        arrived[0, col_step] = bundle[1]
        passed[1, col_step] = bundle[2]
    for row_step in (-1, 1):
        bundle = jnp.stack([parcels[row_step, 0], passed[row_step, -1], passed[row_step, 1]])
        bundle = from_behind(bundle, "gy", row_step)
        arrived[row_step, 0] = bundle[0]
        arrived[row_step, -1] = bundle[1]
        arrived[row_step, 1] = bundle[2]
    return arrived


def on_device(map_codes, reward_table, start_cell, agent_task, actions):
    tile_rows, tile_cols = map_codes.shape
    cell_count = tile_rows * tile_cols
    row_moves = jnp.sum((actions == 2).astype(jnp.int32) - (actions == 1).astype(jnp.int32), axis=0)
    col_moves = jnp.sum((actions == 4).astype(jnp.int32) - (actions == 3).astype(jnp.int32), axis=0)
    local_row = start_cell // tile_cols + row_moves
    local_col = start_cell % tile_cols + col_moves
    row_owner = jnp.where(local_row < 0, -1, jnp.where(local_row >= tile_rows, 1, 0))
    col_owner = jnp.where(local_col < 0, -1, jnp.where(local_col >= tile_cols, 1, 0))
    owner_cell = (local_row - row_owner * tile_rows) * tile_cols + (
        local_col - col_owner * tile_cols
    )
    heading = ((row_owner + 1) * 3 + col_owner + 1).astype(jnp.int32)
    heading_hot = (heading[None, :] == jnp.arange(9, dtype=jnp.int32)[:, None]).astype(jnp.int32)
    ranking = jnp.sum(heading_hot * (jnp.cumsum(heading_hot, axis=1) - 1), axis=0)
    payload = jnp.stack([owner_cell, agent_task]).astype(jnp.float32).T
    blank = jnp.stack(
        [jnp.full((9, CAP), -1.0, jnp.float32), jnp.zeros((9, CAP), jnp.float32)], axis=1
    )
    packed = blank.at[heading, :, ranking].set(payload, mode="drop")
    parcels = {
        offset_pair: packed[(offset_pair[0] + 1) * 3 + offset_pair[1] + 1]
        for offset_pair in NEIGHBOURS
    }
    arrived = deliver(parcels)
    arrivals = jnp.stack([arrived[offset_pair] for offset_pair in NEIGHBOURS])
    foreign_cell = arrivals[:, 0].astype(jnp.int32).reshape(-1)
    foreign_task = arrivals[:, 1].astype(jnp.int32).reshape(-1)
    foreign_live = foreign_cell >= 0
    staying = heading == 4
    landing = jnp.concatenate(
        [
            jnp.where(staying, owner_cell, cell_count),
            jnp.where(foreign_live, foreign_cell, cell_count),
        ]
    )
    crowding = jnp.zeros((cell_count + 1,), jnp.float32).at[landing].add(1.0)[:cell_count]
    band_rows = math.gcd(tile_rows, max(1, 8192 // tile_cols))
    code_bands = map_codes.reshape(tile_rows // band_rows, band_rows * tile_cols)

    def lookup_band(band):
        band_hot = (jnp.arange(CODES, dtype=jnp.int32)[:, None] == band[None, :]).astype(
            jnp.float32
        )
        return jnp.dot(reward_table, band_hot, precision=lax.Precision.HIGHEST)

    looked = lax.map(lookup_band, code_bands)
    looked = jnp.transpose(looked, (1, 0, 2)).reshape(reward_table.shape[0], cell_count)
    reward = looked - PENALTY * crowding[None, :]
    reward = reward.reshape(reward_table.shape[0], tile_rows, tile_cols)
    living = (map_codes < CODES - TERMINAL).astype(jnp.float32)[None]
    padded_reward, padded_living = (
        with_halo(reward, (("gx", 2), ("gy", 1)), 4),
        with_halo(living, (("gx", 2), ("gy", 1)), 4),
    )

    def four_sweeps(block_index, current):
        widened = with_halo(current, (("gx", 2), ("gy", 1)), 4)
        for margin in (3, 2, 1, 0):
            widened = sweep_cells(
                margin_part(padded_reward, margin), margin_part(padded_living, margin), widened
            )
        return widened

    values = lax.fori_loop(0, SWEEPS // 4, four_sweeps, reward)
    flat_values = values.reshape(values.shape[0], cell_count)
    answers = flat_values[foreign_task, jnp.where(foreign_live, foreign_cell, 0)]
    answers = jnp.where(foreign_live, answers, 0.0).reshape(8, 1, CAP)
    replies = {}
    for order_index, offset_pair in enumerate(NEIGHBOURS):
        replies[-offset_pair[0], -offset_pair[1]] = answers[order_index]
    returned = deliver(replies)
    back_rows = []
    for heading_index in range(9):
        row_step = heading_index // 3 - 1
        col_step = heading_index % 3 - 1
        if row_step == 0 and col_step == 0:
            back_rows.append(jnp.zeros((CAP,), jnp.float32))
        else:
            back_rows.append(returned[-row_step, -col_step][0])
    back_table = jnp.stack(back_rows)
    far_value = back_table[heading, jnp.minimum(ranking, CAP - 1)]
    own_value = flat_values[agent_task, jnp.clip(owner_cell, 0, cell_count - 1)]
    agent_value = jnp.where(staying, own_value, far_value)
    return (values, agent_value)


def solution(mesh):
    placed = (P("gy", "gx"), P(), P(("gx", "gy")), P(("gx", "gy")), P(None, ("gx", "gy")))
    return jax.shard_map(
        on_device,
        mesh=mesh,
        in_specs=placed,
        out_specs=(P(None, "gy", "gx"), P(("gx", "gy"))),
        check_vma=False,
    )
```

profile of v0, /device:TPU:1, one launch (start us, length us, event | category | flops | bytes accessed | tf_op | source)
XLA Modules:
  0.0 309.7 jit_solution(8156133659644854634)
XLA Ops:
  3.2 2.6 reduce-window.6
  9.1 5.8 %scatter_fusion = f32[1152,2]{1,0:T(8,128)S(1)} fusion(f32[1152,2]{1,0:T(8,128)S(1)} %copy-done.10, s32[2048]{0:T(1024)S(1)} %broadcast_select_fusion.1, f32[2048,2]{1,0:T(8,128)S(1)} %copy.9), kind=kCustom, calls=%fused_computation.4 | custom fusion | bytes 57344
  15.3 8.9 %collective-permute-start.4 = (f32[3,2,128]{2,0,1:T(4,128)S(1)}, f32[3,2,128]{2,0,1:T(4,128)S(1)}, u32[]{:S(2)}, u32[]{:S(2)}) collective-permute-start(f32[3,2,128]{2,0,1:T(4,128)S(1)} %pad_maximum_fusion.12), channel_id=1, source_target_pairs={{0,240},{16,0},{32,16},{48,32},{64,48},{80,64},{96,80},{112,96},{1... | collective-permute-start | bytes 9224 | tf_op jit(solution)/shard_map/ppermute | solution.py:22
  24.6 5.1 %collective-permute-start.13 = (f32[1,256,4]{2,1,0:T(8,128)S(1)}, f32[1,256,4]{2,1,0:T(8,128)S(1)}, u32[]{:S(2)}, u32[]{:S(2)}) collective-permute-start(f32[1,256,4]{2,1,0:T(8,128)S(1)} %get-tuple-element.96), channel_id=1, source_target_pairs={{16,0},{32,16},{48,32},{64,48},{80,64},{96,80},{112,96},{128,112},... | collective-permute-start | bytes 12296 | tf_op jit(solution)/shard_map/ppermute | solution.py:34
  29.8 6.6 %while.20 = (s32[]{:T(128)}, f32[8,4,8192]{2,1,0:T(4,128)S(1)}, s32[8,8192]{1,0:T(8,128)S(1)}, f32[4,64]{1,0:T(4,128)S(1)}, s32[]{:T(128)}) while((s32[]{:T(128)}, f32[8,4,8192]{2,1,0:T(4,128)S(1)}, s32[8,8192]{1,0:T(8,128)S(1)}, f32[4,64]{1,0:T(4,128)S(1)}, s32[]{:T(128)}) %tuple.90), condition=%wide.region_1.0_spmd, body=%wide.region_0.0_spmd.sunk | while | flops 25690112 | bytes 231493 | solution.py:117
  43.6 18.2 %scatter_custom_fusion = f32[65537]{0:T(1024)S(1)} fusion(s32[3072]{0:T(1024)S(1)} %bitcast.108, f32[3072]{0:T(1024)S(1)} %broadcast.245, f32[]{:T(128)} %constant.33.clone.1), kind=kCustom, calls=%fused_computation.43 | custom fusion | flops 3072 | bytes 262152 | tf_op jit(solution)/shard_map/scatter-add | solution.py:107
  62.4 5.1 %collective-permute-start.9 = (f32[4,256,4]{2,1,0:T(8,128)S(1)}, f32[4,256,4]{2,1,0:T(8,128)S(1)}, u32[]{:S(2)}, u32[]{:S(2)}) collective-permute-start(f32[4,256,4]{2,1,0:T(8,128)S(1)} %get-tuple-element.92), channel_id=1, source_target_pairs={{16,0},{32,16},{48,32},{64,48},{80,64},{96,80},{112,96},{128,112},... | collective-permute-start | bytes 49160 | tf_op jit(solution)/shard_map/ppermute | solution.py:34
  67.5 17.1 %collective-permute-done.8 = f32[4,256,4]{2,1,0:T(8,128)S(1)} collective-permute-done((f32[4,256,4]{2,1,0:T(8,128)S(1)}, f32[4,256,4]{2,1,0:T(8,128)S(1)}, u32[]{:S(2)}, u32[]{:S(2)}) %collective-permute-start.8) | collective-permute-done | bytes 16416 | tf_op jit(solution)/shard_map/ppermute | solution.py:31
  84.6 2.3 collective-permute-done.9
  92.0 163.7 %while.21 = (s32[]{:T(128)}, f32[4,256,256]{2,1,0:T(8,128)S(1)}, f32[1,256,256]{2,1,0:T(8,128)}, f32[4,264,264]{2,1,0:T(8,128)S(1)}, f32[1,264,264]{2,1,0:T(8,128)S(1)}, /*index=5*/f32[4,256,256]{2,1,0:T(8,128)}, s32[]{:T(128)}) while((s32[]{:T(128)}, f32[4,256,256]{2,1,0:T(8,128)S(1)}, f32[1,256,256]{2,1,0:T(8,128)}, ...), condition=%wide.region_10.11_spmd, body=%wide.region_9.10_spmd.sunk | while | flops 6767258 | bytes 41261200 | solution.py:135
  92.2 4.3 %collective-permute-start = (f32[4,256,4]{2,1,0:T(8,128)S(1)}, f32[4,256,4]{2,1,0:T(8,128)S(1)}, u32[]{:S(2)}, u32[]{:S(2)}) collective-permute-start(f32[4,256,4]{2,1,0:T(8,128)S(1)} %get-tuple-element.209), channel_id=1, source_target_pairs={{16,0},{32,16},{48,32},{64,48},{80,64},{96,80},{112,96},{128,112},... | collective-permute-start | bytes 49160 | tf_op jit(solution)/shard_map/while/body/eval_jaxpr/ppermute | solution.py:34
  98.5 16.1 %collective-permute-done = f32[4,256,4]{2,1,0:T(8,128)S(1)} collective-permute-done((f32[4,256,4]{2,1,0:T(8,128)S(1)}, f32[4,256,4]{2,1,0:T(8,128)S(1)}, u32[]{:S(2)}, u32[]{:S(2)}) %collective-permute-start) | collective-permute-done | bytes 16416 | tf_op jit(solution)/shard_map/while/body/eval_jaxpr/ppermute | solution.py:34
  114.6 3.2 %collective-permute-done.1 = f32[4,256,4]{2,1,0:T(8,128)S(1)} collective-permute-done((f32[4,256,4]{2,1,0:T(8,128)S(1)}, f32[4,256,4]{2,1,0:T(8,128)S(1)}, u32[]{:S(2)}, u32[]{:S(2)}) %collective-permute-start.1) | collective-permute-done | bytes 16416 | tf_op jit(solution)/shard_map/while/body/eval_jaxpr/ppermute | solution.py:31
  118.6 2.4 collective-permute-start.2
  122.1 2.9 collective-permute-done.3
  126.9 2.0 fusion.58
  133.7 5.4 %collective-permute-start = (f32[4,256,4]{2,1,0:T(8,128)S(1)}, f32[4,256,4]{2,1,0:T(8,128)S(1)}, u32[]{:S(2)}, u32[]{:S(2)}) collective-permute-start(f32[4,256,4]{2,1,0:T(8,128)S(1)} %get-tuple-element.209), channel_id=1, source_target_pairs={{16,0},{32,16},{48,32},{64,48},{80,64},{96,80},{112,96},{128,112},... | collective-permute-start | bytes 49160 | tf_op jit(solution)/shard_map/while/body/eval_jaxpr/ppermute | solution.py:34
  141.2 4.6 %collective-permute-done = f32[4,256,4]{2,1,0:T(8,128)S(1)} collective-permute-done((f32[4,256,4]{2,1,0:T(8,128)S(1)}, f32[4,256,4]{2,1,0:T(8,128)S(1)}, u32[]{:S(2)}, u32[]{:S(2)}) %collective-permute-start) | collective-permute-done | bytes 16416 | tf_op jit(solution)/shard_map/while/body/eval_jaxpr/ppermute | solution.py:34
  145.8 12.7 %collective-permute-done.1 = f32[4,256,4]{2,1,0:T(8,128)S(1)} collective-permute-done((f32[4,256,4]{2,1,0:T(8,128)S(1)}, f32[4,256,4]{2,1,0:T(8,128)S(1)}, u32[]{:S(2)}, u32[]{:S(2)}) %collective-permute-start.1) | collective-permute-done | bytes 16416 | tf_op jit(solution)/shard_map/while/body/eval_jaxpr/ppermute | solution.py:31
  159.3 3.2 %collective-permute-start.2 = (f32[4,4,264]{2,1,0:T(4,128)}, f32[4,4,264]{2,1,0:T(4,128)S(1)}, u32[]{:S(2)}, u32[]{:S(2)}) collective-permute-start(f32[4,4,264]{2,1,0:T(4,128)} %get-tuple-element.211), channel_id=1, source_target_pairs={{1,0},{2,1},{3,2},{4,3},{5,4},{6,5},{7,6},{8,7},{9,8},{10,9},{11,1... | collective-permute-start | bytes 50696 | tf_op jit(solution)/shard_map/while/body/eval_jaxpr/ppermute | solution.py:34
  167.1 2.0 fusion.58
  173.9 7.3 %collective-permute-start = (f32[4,256,4]{2,1,0:T(8,128)S(1)}, f32[4,256,4]{2,1,0:T(8,128)S(1)}, u32[]{:S(2)}, u32[]{:S(2)}) collective-permute-start(f32[4,256,4]{2,1,0:T(8,128)S(1)} %get-tuple-element.209), channel_id=1, source_target_pairs={{16,0},{32,16},{48,32},{64,48},{80,64},{96,80},{112,96},{128,112},... | collective-permute-start | bytes 49160 | tf_op jit(solution)/shard_map/while/body/eval_jaxpr/ppermute | solution.py:34
  183.2 4.6 %collective-permute-done = f32[4,256,4]{2,1,0:T(8,128)S(1)} collective-permute-done((f32[4,256,4]{2,1,0:T(8,128)S(1)}, f32[4,256,4]{2,1,0:T(8,128)S(1)}, u32[]{:S(2)}, u32[]{:S(2)}) %collective-permute-start) | collective-permute-done | bytes 16416 | tf_op jit(solution)/shard_map/while/body/eval_jaxpr/ppermute | solution.py:34
  187.8 13.1 %collective-permute-done.1 = f32[4,256,4]{2,1,0:T(8,128)S(1)} collective-permute-done((f32[4,256,4]{2,1,0:T(8,128)S(1)}, f32[4,256,4]{2,1,0:T(8,128)S(1)}, u32[]{:S(2)}, u32[]{:S(2)}) %collective-permute-start.1) | collective-permute-done | bytes 16416 | tf_op jit(solution)/shard_map/while/body/eval_jaxpr/ppermute | solution.py:31
  214.3 7.8 %collective-permute-start = (f32[4,256,4]{2,1,0:T(8,128)S(1)}, f32[4,256,4]{2,1,0:T(8,128)S(1)}, u32[]{:S(2)}, u32[]{:S(2)}) collective-permute-start(f32[4,256,4]{2,1,0:T(8,128)S(1)} %get-tuple-element.209), channel_id=1, source_target_pairs={{16,0},{32,16},{48,32},{64,48},{80,64},{96,80},{112,96},{128,112},... | collective-permute-start | bytes 49160 | tf_op jit(solution)/shard_map/while/body/eval_jaxpr/ppermute | solution.py:34
  224.2 4.6 %collective-permute-done = f32[4,256,4]{2,1,0:T(8,128)S(1)} collective-permute-done((f32[4,256,4]{2,1,0:T(8,128)S(1)}, f32[4,256,4]{2,1,0:T(8,128)S(1)}, u32[]{:S(2)}, u32[]{:S(2)}) %collective-permute-start) | collective-permute-done | bytes 16416 | tf_op jit(solution)/shard_map/while/body/eval_jaxpr/ppermute | solution.py:34
  228.8 13.5 %collective-permute-done.1 = f32[4,256,4]{2,1,0:T(8,128)S(1)} collective-permute-done((f32[4,256,4]{2,1,0:T(8,128)S(1)}, f32[4,256,4]{2,1,0:T(8,128)S(1)}, u32[]{:S(2)}, u32[]{:S(2)}) %collective-permute-start.1) | collective-permute-done | bytes 16416 | tf_op jit(solution)/shard_map/while/body/eval_jaxpr/ppermute | solution.py:31
  256.4 9.3 %gather_fusion.1 = f32[1024]{0:T(1024)S(1)} fusion(f32[4,65536]{1,0:T(4,128)S(1)} %bitcast.89, s32[1024]{0:T(1024)S(1)} %bitcast.92), kind=kCustom, calls=%fused_computation.1 | custom fusion | bytes 16384 | tf_op jit(solution)/shard_map/gather | solution.py:137
  265.8 6.3 %collective-permute-start.16 = (f32[3,1,128]{2,1,0:T(1,128)S(1)}, f32[3,1,128]{2,1,0:T(1,128)S(1)}, u32[]{:S(2)}, u32[]{:S(2)}) collective-permute-start(f32[3,1,128]{2,1,0:T(1,128)S(1)} %pad_maximum_fusion.16), channel_id=1, source_target_pairs={{0,240},{16,0},{32,16},{48,32},{64,48},{80,64},{96,80},{112,96},{1... | collective-permute-start | bytes 4616 | tf_op jit(solution)/shard_map/ppermute | solution.py:22
  272.1 17.7 %gather_fusion = f32[2048]{0:T(1024)S(1)} fusion(f32[4,65536]{1,0:T(4,128)S(1)} %bitcast.90, s32[2048]{0:T(1024)S(1)} %get-tuple-element.80), kind=kCustom, calls=%fused_computation | custom fusion | bytes 32768 | tf_op jit(solution)/shard_map/gather | solution.py:153
  289.9 5.0 %collective-permute-start.19 = (f32[3,1,128]{2,1,0:T(1,128)S(1)}, f32[3,1,128]{2,1,0:T(1,128)S(1)}, u32[]{:S(2)}, u32[]{:S(2)}) collective-permute-start(f32[3,1,128]{2,1,0:T(1,128)S(1)} %pad_maximum_fusion.19), channel_id=1, source_target_pairs={{0,15},{1,0},{2,1},{3,2},{4,3},{5,4},{6,5},{7,6},{8,7},{9,8},{10,9... | collective-permute-start | bytes 4616 | tf_op jit(solution)/shard_map/ppermute | solution.py:22
  296.1 13.1 %gather_fusion.2 = f32[2048]{0:T(1024)S(1)} fusion(f32[9,128]{1,0:T(8,128)S(1)} %stack.51, s32[2048]{0:T(1024)S(1)} %bitcast.91), kind=kCustom, calls=%fused_computation.2 | custom fusion | bytes 32768 | tf_op jit(solution)/shard_map/gather | solution.py:152
  (231 shorter events, 81.8 us)
Async XLA Ops:
  15.3 21.8 %collective-permute-start.4 = (f32[3,2,128]{2,0,1:T(4,128)S(1)}, f32[3,2,128]{2,0,1:T(4,128)S(1)}, u32[]{:S(2)}, u32[]{:S(2)}) collective-permute-start(f32[3,2,128]{2,0,1:T(4,128)S(1)} %pad_maximum_fusion.12), channel_id=1, source_target_pairs={{0,240},{16,0},{32,16},{48,32},{64,48},{80,64},{96,80},{112,96},{1... | collective-permute-start | bytes 9224 | tf_op jit(solution)/shard_map/ppermute | solution.py:22
  24.3 12.9 %collective-permute-start.5 = (f32[3,2,128]{2,0,1:T(4,128)S(1)}, f32[3,2,128]{2,0,1:T(4,128)S(1)}, u32[]{:S(2)}, u32[]{:S(2)}) collective-permute-start(f32[3,2,128]{2,0,1:T(4,128)S(1)} %pad_maximum_fusion.13), channel_id=1, source_target_pairs={{0,16},{16,32},{32,48},{48,64},{64,80},{80,96},{96,112},{112,128},... | collective-permute-start | bytes 9224 | tf_op jit(solution)/shard_map/ppermute | solution.py:22
  24.5 14.6 %collective-permute-start.12 = (f32[1,256,4]{2,1,0:T(8,128)S(1)}, f32[1,256,4]{2,1,0:T(8,128)S(1)}, u32[]{:S(2)}, u32[]{:S(2)}) collective-permute-start(f32[1,256,4]{2,1,0:T(8,128)S(1)} %get-tuple-element.95), channel_id=1, source_target_pairs={{0,16},{16,32},{32,48},{48,64},{64,80},{80,96},{96,112},{112,128},... | collective-permute-start | bytes 12296 | tf_op jit(solution)/shard_map/ppermute | solution.py:31
  24.6 14.5 %collective-permute-start.13 = (f32[1,256,4]{2,1,0:T(8,128)S(1)}, f32[1,256,4]{2,1,0:T(8,128)S(1)}, u32[]{:S(2)}, u32[]{:S(2)}) collective-permute-start(f32[1,256,4]{2,1,0:T(8,128)S(1)} %get-tuple-element.96), channel_id=1, source_target_pairs={{16,0},{32,16},{48,32},{64,48},{80,64},{96,80},{112,96},{128,112},... | collective-permute-start | bytes 12296 | tf_op jit(solution)/shard_map/ppermute | solution.py:34
  37.2 5.7 %collective-permute-start.7 = (f32[3,2,128]{2,0,1:T(4,128)S(1)}, f32[3,2,128]{2,0,1:T(4,128)S(1)}, u32[]{:S(2)}, u32[]{:S(2)}) collective-permute-start(f32[3,2,128]{2,0,1:T(4,128)S(1)} %pad_maximum_fusion.15), channel_id=1, source_target_pairs={{0,1},{1,2},{2,3},{3,4},{4,5},{5,6},{6,7},{7,8},{8,9},{9,10},{10,1... | collective-permute-start | bytes 9224 | tf_op jit(solution)/shard_map/ppermute | solution.py:22
  39.0 3.9 %collective-permute-start.6 = (f32[3,2,128]{2,0,1:T(4,128)S(1)}, f32[3,2,128]{2,0,1:T(4,128)S(1)}, u32[]{:S(2)}, u32[]{:S(2)}) collective-permute-start(f32[3,2,128]{2,0,1:T(4,128)S(1)} %pad_maximum_fusion.14), channel_id=1, source_target_pairs={{0,15},{1,0},{2,1},{3,2},{4,3},{5,4},{6,5},{7,6},{8,7},{9,8},{10,9... | collective-permute-start | bytes 9224 | tf_op jit(solution)/shard_map/ppermute | solution.py:22
  39.2 50.6 %collective-permute-start.14 = (f32[1,4,264]{2,1,0:T(4,128)S(1)}, f32[1,4,264]{2,1,0:T(4,128)S(1)}, u32[]{:S(2)}, u32[]{:S(2)}) collective-permute-start(f32[1,4,264]{2,1,0:T(4,128)S(1)} %get-tuple-element.93), channel_id=1, source_target_pairs={{0,1},{1,2},{2,3},{3,4},{4,5},{5,6},{6,7},{7,8},{8,9},{9,10},{10,1... | collective-permute-start | bytes 12680 | tf_op jit(solution)/shard_map/ppermute | solution.py:31
  40.9 48.9 %collective-permute-start.15 = (f32[1,4,264]{2,1,0:T(4,128)S(1)}, f32[1,4,264]{2,1,0:T(4,128)S(1)}, u32[]{:S(2)}, u32[]{:S(2)}) collective-permute-start(f32[1,4,264]{2,1,0:T(4,128)S(1)} %get-tuple-element.94), channel_id=1, source_target_pairs={{1,0},{2,1},{3,2},{4,3},{5,4},{6,5},{7,6},{8,7},{9,8},{10,9},{11,1... | collective-permute-start | bytes 12680 | tf_op jit(solution)/shard_map/ppermute | solution.py:34
  62.3 22.3 %collective-permute-start.8 = (f32[4,256,4]{2,1,0:T(8,128)S(1)}, f32[4,256,4]{2,1,0:T(8,128)S(1)}, u32[]{:S(2)}, u32[]{:S(2)}) collective-permute-start(f32[4,256,4]{2,1,0:T(8,128)S(1)} %get-tuple-element.91), channel_id=1, source_target_pairs={{0,16},{16,32},{32,48},{48,64},{64,80},{80,96},{96,112},{112,128},... | collective-permute-start | bytes 49160 | tf_op jit(solution)/shard_map/ppermute | solution.py:31
  62.4 24.6 %collective-permute-start.9 = (f32[4,256,4]{2,1,0:T(8,128)S(1)}, f32[4,256,4]{2,1,0:T(8,128)S(1)}, u32[]{:S(2)}, u32[]{:S(2)}) collective-permute-start(f32[4,256,4]{2,1,0:T(8,128)S(1)} %get-tuple-element.92), channel_id=1, source_target_pairs={{16,0},{32,16},{48,32},{64,48},{80,64},{96,80},{112,96},{128,112},... | collective-permute-start | bytes 49160 | tf_op jit(solution)/shard_map/ppermute | solution.py:34
  87.0 3.3 %collective-permute-start.10 = (f32[4,4,264]{2,1,0:T(4,128)S(1)}, f32[4,4,264]{2,1,0:T(4,128)S(1)}, u32[]{:S(2)}, u32[]{:S(2)}) collective-permute-start(f32[4,4,264]{2,1,0:T(4,128)S(1)} %get-tuple-element.89), channel_id=1, source_target_pairs={{0,1},{1,2},{2,3},{3,4},{4,5},{5,6},{6,7},{7,8},{8,9},{9,10},{10,1... | collective-permute-start | bytes 50696 | tf_op jit(solution)/shard_map/ppermute | solution.py:31
  88.0 3.3 %collective-permute-start.11 = (f32[4,4,264]{2,1,0:T(4,128)S(1)}, f32[4,4,264]{2,1,0:T(4,128)S(1)}, u32[]{:S(2)}, u32[]{:S(2)}) collective-permute-start(f32[4,4,264]{2,1,0:T(4,128)S(1)} %get-tuple-element.90), channel_id=1, source_target_pairs={{1,0},{2,1},{3,2},{4,3},{5,4},{6,5},{7,6},{8,7},{9,8},{10,9},{11,1... | collective-permute-start | bytes 50696 | tf_op jit(solution)/shard_map/ppermute | solution.py:34
  92.2 22.4 %collective-permute-start = (f32[4,256,4]{2,1,0:T(8,128)S(1)}, f32[4,256,4]{2,1,0:T(8,128)S(1)}, u32[]{:S(2)}, u32[]{:S(2)}) collective-permute-start(f32[4,256,4]{2,1,0:T(8,128)S(1)} %get-tuple-element.209), channel_id=1, source_target_pairs={{16,0},{32,16},{48,32},{64,48},{80,64},{96,80},{112,96},{128,112},... | collective-permute-start | bytes 49160 | tf_op jit(solution)/shard_map/while/body/eval_jaxpr/ppermute | solution.py:34
  96.4 21.4 %collective-permute-start.1 = (f32[4,256,4]{2,1,0:T(8,128)S(1)}, f32[4,256,4]{2,1,0:T(8,128)S(1)}, u32[]{:S(2)}, u32[]{:S(2)}) collective-permute-start(f32[4,256,4]{2,1,0:T(8,128)S(1)} %get-tuple-element.210), channel_id=1, source_target_pairs={{0,16},{16,32},{32,48},{48,64},{64,80},{80,96},{96,112},{112,128},... | collective-permute-start | bytes 49160 | tf_op jit(solution)/shard_map/while/body/eval_jaxpr/ppermute | solution.py:31
  118.6 3.5 %collective-permute-start.2 = (f32[4,4,264]{2,1,0:T(4,128)}, f32[4,4,264]{2,1,0:T(4,128)S(1)}, u32[]{:S(2)}, u32[]{:S(2)}) collective-permute-start(f32[4,4,264]{2,1,0:T(4,128)} %get-tuple-element.211), channel_id=1, source_target_pairs={{1,0},{2,1},{3,2},{4,3},{5,4},{6,5},{7,6},{8,7},{9,8},{10,9},{11,1... | collective-permute-start | bytes 50696 | tf_op jit(solution)/shard_map/while/body/eval_jaxpr/ppermute | solution.py:34
  121.0 4.0 %collective-permute-start.3 = (f32[4,4,264]{2,1,0:T(4,128)S(1)}, f32[4,4,264]{2,1,0:T(4,128)}, u32[]{:S(2)}, u32[]{:S(2)}) collective-permute-start(f32[4,4,264]{2,1,0:T(4,128)S(1)} %get-tuple-element.212), channel_id=1, source_target_pairs={{0,1},{1,2},{2,3},{3,4},{4,5},{5,6},{6,7},{7,8},{8,9},{9,10},{10,1... | collective-permute-start | bytes 50696 | tf_op jit(solution)/shard_map/while/body/eval_jaxpr/ppermute | solution.py:31
  133.7 12.1 %collective-permute-start = (f32[4,256,4]{2,1,0:T(8,128)S(1)}, f32[4,256,4]{2,1,0:T(8,128)S(1)}, u32[]{:S(2)}, u32[]{:S(2)}) collective-permute-start(f32[4,256,4]{2,1,0:T(8,128)S(1)} %get-tuple-element.209), channel_id=1, source_target_pairs={{16,0},{32,16},{48,32},{64,48},{80,64},{96,80},{112,96},{128,112},... | collective-permute-start | bytes 49160 | tf_op jit(solution)/shard_map/while/body/eval_jaxpr/ppermute | solution.py:34
  139.1 19.3 %collective-permute-start.1 = (f32[4,256,4]{2,1,0:T(8,128)S(1)}, f32[4,256,4]{2,1,0:T(8,128)S(1)}, u32[]{:S(2)}, u32[]{:S(2)}) collective-permute-start(f32[4,256,4]{2,1,0:T(8,128)S(1)} %get-tuple-element.210), channel_id=1, source_target_pairs={{0,16},{16,32},{32,48},{48,64},{64,80},{80,96},{96,112},{112,128},... | collective-permute-start | bytes 49160 | tf_op jit(solution)/shard_map/while/body/eval_jaxpr/ppermute | solution.py:31
  159.3 4.3 %collective-permute-start.2 = (f32[4,4,264]{2,1,0:T(4,128)}, f32[4,4,264]{2,1,0:T(4,128)S(1)}, u32[]{:S(2)}, u32[]{:S(2)}) collective-permute-start(f32[4,4,264]{2,1,0:T(4,128)} %get-tuple-element.211), channel_id=1, source_target_pairs={{1,0},{2,1},{3,2},{4,3},{5,4},{6,5},{7,6},{8,7},{9,8},{10,9},{11,1... | collective-permute-start | bytes 50696 | tf_op jit(solution)/shard_map/while/body/eval_jaxpr/ppermute | solution.py:34
  162.5 2.7 collective-permute-start.3
  173.9 14.0 %collective-permute-start = (f32[4,256,4]{2,1,0:T(8,128)S(1)}, f32[4,256,4]{2,1,0:T(8,128)S(1)}, u32[]{:S(2)}, u32[]{:S(2)}) collective-permute-start(f32[4,256,4]{2,1,0:T(8,128)S(1)} %get-tuple-element.209), channel_id=1, source_target_pairs={{16,0},{32,16},{48,32},{64,48},{80,64},{96,80},{112,96},{128,112},... | collective-permute-start | bytes 49160 | tf_op jit(solution)/shard_map/while/body/eval_jaxpr/ppermute | solution.py:34
  181.1 19.7 %collective-permute-start.1 = (f32[4,256,4]{2,1,0:T(8,128)S(1)}, f32[4,256,4]{2,1,0:T(8,128)S(1)}, u32[]{:S(2)}, u32[]{:S(2)}) collective-permute-start(f32[4,256,4]{2,1,0:T(8,128)S(1)} %get-tuple-element.210), channel_id=1, source_target_pairs={{0,16},{16,32},{32,48},{48,64},{64,80},{80,96},{96,112},{112,128},... | collective-permute-start | bytes 49160 | tf_op jit(solution)/shard_map/while/body/eval_jaxpr/ppermute | solution.py:31
  201.7 3.5 %collective-permute-start.2 = (f32[4,4,264]{2,1,0:T(4,128)}, f32[4,4,264]{2,1,0:T(4,128)S(1)}, u32[]{:S(2)}, u32[]{:S(2)}) collective-permute-start(f32[4,4,264]{2,1,0:T(4,128)} %get-tuple-element.211), channel_id=1, source_target_pairs={{1,0},{2,1},{3,2},{4,3},{5,4},{6,5},{7,6},{8,7},{9,8},{10,9},{11,1... | collective-permute-start | bytes 50696 | tf_op jit(solution)/shard_map/while/body/eval_jaxpr/ppermute | solution.py:34
  202.9 2.8 collective-permute-start.3
  214.3 14.4 %collective-permute-start = (f32[4,256,4]{2,1,0:T(8,128)S(1)}, f32[4,256,4]{2,1,0:T(8,128)S(1)}, u32[]{:S(2)}, u32[]{:S(2)}) collective-permute-start(f32[4,256,4]{2,1,0:T(8,128)S(1)} %get-tuple-element.209), channel_id=1, source_target_pairs={{16,0},{32,16},{48,32},{64,48},{80,64},{96,80},{112,96},{128,112},... | collective-permute-start | bytes 49160 | tf_op jit(solution)/shard_map/while/body/eval_jaxpr/ppermute | solution.py:34
  222.1 20.2 %collective-permute-start.1 = (f32[4,256,4]{2,1,0:T(8,128)S(1)}, f32[4,256,4]{2,1,0:T(8,128)S(1)}, u32[]{:S(2)}, u32[]{:S(2)}) collective-permute-start(f32[4,256,4]{2,1,0:T(8,128)S(1)} %get-tuple-element.210), channel_id=1, source_target_pairs={{0,16},{16,32},{32,48},{48,64},{64,80},{80,96},{96,112},{112,128},... | collective-permute-start | bytes 49160 | tf_op jit(solution)/shard_map/while/body/eval_jaxpr/ppermute | solution.py:31
  243.1 3.5 %collective-permute-start.2 = (f32[4,4,264]{2,1,0:T(4,128)}, f32[4,4,264]{2,1,0:T(4,128)S(1)}, u32[]{:S(2)}, u32[]{:S(2)}) collective-permute-start(f32[4,4,264]{2,1,0:T(4,128)} %get-tuple-element.211), channel_id=1, source_target_pairs={{1,0},{2,1},{3,2},{4,3},{5,4},{6,5},{7,6},{8,7},{9,8},{10,9},{11,1... | collective-permute-start | bytes 50696 | tf_op jit(solution)/shard_map/while/body/eval_jaxpr/ppermute | solution.py:34
  244.3 2.9 collective-permute-start.3
  265.8 24.0 %collective-permute-start.16 = (f32[3,1,128]{2,1,0:T(1,128)S(1)}, f32[3,1,128]{2,1,0:T(1,128)S(1)}, u32[]{:S(2)}, u32[]{:S(2)}) collective-permute-start(f32[3,1,128]{2,1,0:T(1,128)S(1)} %pad_maximum_fusion.16), channel_id=1, source_target_pairs={{0,240},{16,0},{32,16},{48,32},{64,48},{80,64},{96,80},{112,96},{1... | collective-permute-start | bytes 4616 | tf_op jit(solution)/shard_map/ppermute | solution.py:22
  272.1 17.8 %collective-permute-start.17 = (f32[3,1,128]{2,1,0:T(1,128)S(1)}, f32[3,1,128]{2,1,0:T(1,128)S(1)}, u32[]{:S(2)}, u32[]{:S(2)}) collective-permute-start(f32[3,1,128]{2,1,0:T(1,128)S(1)} %pad_maximum_fusion.17), channel_id=1, source_target_pairs={{0,16},{16,32},{32,48},{48,64},{64,80},{80,96},{96,112},{112,128},... | collective-permute-start | bytes 4616 | tf_op jit(solution)/shard_map/ppermute | solution.py:22
  289.9 5.8 %collective-permute-start.19 = (f32[3,1,128]{2,1,0:T(1,128)S(1)}, f32[3,1,128]{2,1,0:T(1,128)S(1)}, u32[]{:S(2)}, u32[]{:S(2)}) collective-permute-start(f32[3,1,128]{2,1,0:T(1,128)S(1)} %pad_maximum_fusion.19), channel_id=1, source_target_pairs={{0,15},{1,0},{2,1},{3,2},{4,3},{5,4},{6,5},{7,6},{8,7},{9,8},{10,9... | collective-permute-start | bytes 4616 | tf_op jit(solution)/shard_map/ppermute | solution.py:22
  294.9 1.2 collective-permute-start.18
  (36 other events, 330.0 us)
where the time goes:
time: 312 us; the launch traced here: 310 us
  waiting for transfers between devices  102 us (33%)
  other arithmetic  75.7 us (24%)
  starting transfers between devices  72.8 us (23%)
  local copies, waits for them, and re-layouts  50.8 us (16%)
  matrix products  6.2 us (2%)
    ppermute x12, waiting for transfers between devices, with_halo(): lax.ppermute(lax.slice_in_dim(block, block.shape[dim] - width, None, axis...  65.6 us
    ppermute x12, starting transfers between devices, with_halo(): lax.ppermute(lax.slice_in_dim(block, 0, width, axis=dim), axis, backward)  46.6 us
    ppermute x12, waiting for transfers between devices, with_halo(): lax.ppermute(lax.slice_in_dim(block, 0, width, axis=dim), axis, backward)  35.7 us
    add x16, other arithmetic, sweep_cells(): return reward + GAMMA * living * highest  26 us
    ppermute x8, starting transfers between devices, from_behind(): return lax.ppermute(value, axis, pairs)  22.2 us
    scatter-add x1, other arithmetic, on_device(): jnp.zeros((cell_count + 1,), jnp.float32).at[landing].add(1.0)[:cell_count]  18.2 us
    gather x1, local copies, waits for them, and re-layouts, on_device(): own_value = flat_values[agent_task, jnp.clip(owner_cell, 0, cell_count - 1)]  17.7 us
    gather x1, local copies, waits for them, and re-layouts, on_device(): far_value = back_table[heading, jnp.minimum(ranking, CAP - 1)]  13.1 us
  transfers between devices with their start and end apart: 32, of which 22 were waited for; matrix products, arithmetic and copies ran while one was open for 18% of the time, Pallas kernels for 0%

commit v1 on v0

v1 whole, which is shorter than its diff:
```python
import functools

import jax
import jax.numpy as jnp
from jax import lax
from jax.experimental import pallas as pl
from jax.experimental.pallas import tpu as pltpu
from jax.sharding import PartitionSpec as P

SWEEPS = 16
CODES = 64
TERMINAL = 2
GAMMA = 0.95
PENALTY = 0.5
NEIGHBOURS = ((-1, -1), (-1, 0), (-1, 1), (0, -1), (0, 1), (1, -1), (1, 0), (1, 1))

TILE = 256
HALO = 32
EXT = TILE + 2 * HALO
ROWS = EXT // 8
COLS = 10
LANES = 128
TASK_LANES = 32
WIDE = COLS * LANES
AGENTS = 2048
STRIDE = 512
EDGE = 48

F32 = jnp.float32
BF16 = jnp.bfloat16
I32 = jnp.int32
MESH = pl.DeviceIdType.MESH
NT = (((1,), (1,)), ((), ()))
NN = (((1,), (0,)), ((), ()))


def dot(a, b, dims=NN):
    return lax.dot_general(a, b, dims, preferred_element_type=F32)


def iota(shape, dim):
    return lax.broadcasted_iota(I32, shape, dim)


def hot(values, first, count):
    cells = iota((count, values.shape[1]), 0) + first
    return jnp.where(cells == values, 1.0, 0.0).astype(BF16)


def edge_hot(cols):
    slot = iota((LANES, cols.shape[1]), 0)
    place = jnp.where(cols < EDGE, cols, cols - (EXT - EDGE) + EDGE)
    place = jnp.where((cols >= EDGE) & (cols < EXT - EDGE), -1, place)
    place = jnp.where((cols < 0) | (cols >= EXT), -1, place)
    return jnp.where(slot == place, 1.0, 0.0).astype(BF16)


def exchange_kernel(
    start_hbm, act_hbm, codes_hbm,
    cells_out, lists_out, n_out, s_out, w_out, e_out, corner_out,
    start_v, act_v, codes_v, w_send, e_send, corner_send, local_sem, send_sem, recv_sem,
):
    gx = lax.axis_index("gx")
    gy = lax.axis_index("gy")

    def device(step):
        return (lax.rem(gx + step[1] + 16, 16), lax.rem(gy + step[0] + 16, 16))

    loads = [
        pltpu.make_async_copy(codes_hbm, codes_v, local_sem.at[0]),
        pltpu.make_async_copy(act_hbm, act_v, local_sem.at[1]),
        pltpu.make_async_copy(start_hbm, start_v, local_sem.at[2]),
    ]
    for load in loads:
        load.start()
    barrier = pltpu.get_barrier_semaphore()
    for step in NEIGHBOURS:
        pl.semaphore_signal(barrier, inc=1, device_id=device(step), device_id_type=MESH)

    loads[1].wait()
    loads[2].wait()
    act = act_v[...]
    row = start_v[...] // TILE + HALO
    col = start_v[...] % TILE + HALO
    row += jnp.sum((act == 2).astype(I32) - (act == 1).astype(I32), axis=0, keepdims=True)
    col += jnp.sum((act == 4).astype(I32) - (act == 3).astype(I32), axis=0, keepdims=True)
    cells_out[...] = row * STRIDE + col

    loads[0].wait()
    lane = iota((64, LANES), 1)
    west = jnp.zeros((64, LANES), I32)
    east = jnp.zeros((64, LANES), I32)
    for q in range(4):
        mine = (lane >= 32 * q) & (lane < 32 * q + 32)
        rows = pl.ds(64 * q, 64)
        low = codes_v[rows, 0:128]
        high = codes_v[rows, 128:256]
        west = jnp.where(mine, pltpu.roll(low, 32 * q, 1), west)
        east = jnp.where(mine, pltpu.roll(high, (32 * q + 32) % 128, 1), east)
    w_send[...] = west
    e_send[...] = east
    for k, (r, c) in enumerate(((-1, -1), (-1, 1), (1, -1), (1, 1))):
        piece = jnp.zeros((8, LANES), I32)
        for q in range(4):
            mine = (lane[0:8] >= 32 * q) & (lane[0:8] < 32 * q + 32)
            rows = pl.ds((0 if r < 0 else 224) + 8 * q, 8)
            if c < 0:
                part = pltpu.roll(codes_v[rows, 0:128], 32 * q, 1)
            else:
                part = pltpu.roll(codes_v[rows, 128:256], (32 * q + 32) % 128, 1)
            piece = jnp.where(mine, part, piece)
        corner_send[k] = piece

    pl.semaphore_wait(barrier, 8)
    copies = []

    def send(source, target, step):
        k = len(copies)
        copy = pltpu.make_async_remote_copy(
            source, target, send_sem.at[k], recv_sem.at[k],
            device_id=device(step), device_id_type=MESH,
        )
        copy.start()
        copies.append(copy)

    send(w_send, e_out, (0, -1))
    send(e_send, w_out, (0, 1))
    for k, step in enumerate(((-1, -1), (-1, 1), (1, -1), (1, 1))):
        send(corner_send.at[k], corner_out.at[3 - k], step)
    for k, step in enumerate(NEIGHBOURS):
        send(cells_out, lists_out.at[7 - k], step)
    send(codes_v.at[pl.ds(0, 32)], s_out, (-1, 0))
    send(codes_v.at[pl.ds(224, 32)], n_out, (1, 0))
    for copy in copies:
        copy.wait()


def exchange(codes, start, actions):
    return pl.pallas_call(
        exchange_kernel,
        out_shape=(
            jax.ShapeDtypeStruct((1, AGENTS), I32),
            jax.ShapeDtypeStruct((8, 1, AGENTS), I32),
            jax.ShapeDtypeStruct((32, TILE), I32),
            jax.ShapeDtypeStruct((32, TILE), I32),
            jax.ShapeDtypeStruct((64, LANES), I32),
            jax.ShapeDtypeStruct((64, LANES), I32),
            jax.ShapeDtypeStruct((4, 8, LANES), I32),
        ),
        in_specs=[pl.BlockSpec(memory_space=pl.ANY)] * 3,
        out_specs=[pl.BlockSpec(memory_space=pltpu.VMEM)] * 7,
        scratch_shapes=[
            pltpu.VMEM((1, AGENTS), I32),
            pltpu.VMEM((16, AGENTS), I32),
            pltpu.VMEM((TILE, TILE), I32),
            pltpu.VMEM((64, LANES), I32),
            pltpu.VMEM((64, LANES), I32),
            pltpu.VMEM((4, 8, LANES), I32),
            pltpu.SemaphoreType.DMA((3,)),
            pltpu.SemaphoreType.DMA((16,)),
            pltpu.SemaphoreType.DMA((16,)),
        ],
        compiler_params=pltpu.CompilerParams(collective_id=0, has_side_effects=True),
        name="exchange",
    )(start, actions, codes)


def frame_kernel(
    cells_ref, lists_ref, n_ref, s_ref, w_ref, e_ref, corner_ref, codes_ref, table_ref, task_ref,
    values_out, agent_out,
    codes_v, count_v, reward_v, decay_v, val_a, val_b, natural_v, picked_v,
    index_v, index_s, out_sem, index_sem,
):
    cells = cells_ref[...]
    row = cells // STRIDE
    col = cells % STRIDE

    block = (row * 1639) >> 16
    inner = row - block * ROWS
    group = (col * 6554) >> 16
    place = ((inner + 1) * COLS + (col - group * COLS)) * 8 + block
    lane_of = task_ref[...] * TASK_LANES + group
    for k in range(16):
        index_v[k : k + 1, :] = place[:, k * LANES : (k + 1) * LANES]
    to_smem = pltpu.make_async_copy(index_v, index_s, index_sem)
    to_smem.start()

    lists = [lists_ref[k] for k in range(8)]
    rows_in = []
    cols_in = []
    for k, (r, c) in enumerate(NEIGHBOURS):
        rows_in.append(lists[k] // STRIDE + r * TILE)
        cols_in.append(lists[k] % STRIDE + c * TILE)
    row_hot = hot(row, 0, EXT)

    def add(k, first, rows, part, fresh=False):
        band = pl.ds(first, rows)
        for c in range(part.shape[1] // LANES):
            piece = part[:, c * LANES : (c + 1) * LANES]
            count_v[k + c, band, :] = piece if fresh else count_v[k + c, band, :] + piece

    def inside(columns):
        columns = jnp.where((columns >= EDGE) & (columns < EXT - EDGE), columns - EDGE, -1)
        return hot(columns, 0, 256)

    add(0, 0, EXT, dot(row_hot, inside(col), NT), True)
    sides = jnp.concatenate([row_hot, hot(rows_in[3], 0, EXT), hot(rows_in[4], 0, EXT)], axis=1)
    side_cols = jnp.concatenate([edge_hot(col), edge_hot(cols_in[3]), edge_hot(cols_in[4])], axis=1)
    add(2, 0, EXT, dot(sides, side_cols, NT), True)
    for first, west, middle, east in ((0, 0, 1, 2), (EXT - EDGE, 5, 6, 7)):
        near = hot(rows_in[middle], first, EDGE)
        add(0, first, EDGE, dot(near, inside(cols_in[middle]), NT))
        all_rows = jnp.concatenate(
            [near, hot(rows_in[west], first, EDGE), hot(rows_in[east], first, EDGE)], axis=1
        )
        all_cols = jnp.concatenate(
            [edge_hot(cols_in[middle]), edge_hot(cols_in[west]), edge_hot(cols_in[east])], axis=1
        )
        add(2, first, EDGE, dot(all_rows, all_cols, NT))

    for c in range(2):
        part = pl.ds(c * LANES, LANES)
        codes_v[c, 0:32, :] = n_ref[:, part].astype(F32)
        codes_v[c, 32:288, :] = codes_ref[:, part].astype(F32)
        codes_v[c, 288:320, :] = s_ref[:, part].astype(F32)
    lane = iota((64, LANES), 1)
    for q in range(4):
        west = pltpu.roll(w_ref[...], (128 - 32 * q) % 128, 1)
        east = pltpu.roll(e_ref[...], (160 - 32 * q) % 128, 1)
        both = jnp.where(lane < 32, west, jnp.where(lane < 64, east, 0))
        codes_v[2, 32 + 64 * q : 96 + 64 * q, :] = both.astype(F32)
        for first, pair in ((0, 0), (288, 2)):
            west = pltpu.roll(corner_ref[pair], (128 - 32 * q) % 128, 1)
            east = pltpu.roll(corner_ref[pair + 1], (160 - 32 * q) % 128, 1)
            both = jnp.where(lane[0:8] < 32, west, jnp.where(lane[0:8] < 64, east, 0))
            codes_v[2, first + 8 * q : first + 8 * q + 8, :] = both.astype(F32)

    out_lane = iota((384, WIDE), 1)
    column = (out_lane % TASK_LANES) * COLS + out_lane // LANES
    slot = iota((384, WIDE), 0)
    code_col = jnp.where(slot < 256, slot + HALO, jnp.where(slot < 288, slot - 256, slot))
    code_col = jnp.where(slot < 320, code_col, -1)
    spread_codes = jnp.where(code_col == column, 1.0, 0.0).astype(BF16)
    count_col = jnp.where(slot < 224, slot + EDGE, -1)
    count_col = jnp.where(slot >= 256, slot - 256, count_col)
    count_col = jnp.where(slot >= 256 + EDGE, slot - 256 - EDGE + EXT - EDGE, count_col)
    count_col = jnp.where(slot >= 256 + 2 * EDGE, -1, count_col)
    spread_counts = jnp.where(count_col == column, 1.0, 0.0).astype(BF16)

    def interleaved(ref):
        return jnp.concatenate(
            [
                jnp.concatenate([ref[c, pl.ds(i, 8, stride=ROWS), :] for i in range(ROWS)], axis=0)
                for c in range(3)
            ],
            axis=1,
        )

    counts = interleaved(count_v)
    high = jnp.floor(counts * (1.0 / 128.0))
    low = counts - high * 128.0
    minus = dot((high * (-128.0 * PENALTY)).astype(BF16), spread_counts)
    minus += dot((low * -PENALTY).astype(BF16), spread_counts)
    wide = dot(interleaved(codes_v).astype(BF16), spread_codes)

    lane8 = iota((8, LANES), 1)
    table = []
    for k in range(2):
        pair = jnp.concatenate([table_ref[2 * k : 2 * k + 1, :], table_ref[2 * k + 1 : 2 * k + 2, :]], axis=1)
        table.append(jnp.broadcast_to(pair, (8, LANES)))
    shift = (lane8 // TASK_LANES % 2) * CODES
    for i in range(ROWS):
        for j in range(COLS):
            code = wide[8 * i : 8 * i + 8, LANES * j : LANES * (j + 1)].astype(I32)
            at = code + shift
            found = jnp.where(
                lane8 < 64,
                jnp.take_along_axis(table[0], at, axis=1),
                jnp.take_along_axis(table[1], at, axis=1),
            )
            reward = found + minus[8 * i : 8 * i + 8, LANES * j : LANES * (j + 1)]
            spot = pl.ds((i * COLS + j) * 8, 8)
            reward_v[spot, :] = reward
            decay_v[spot, :] = jnp.where(code < CODES - TERMINAL, GAMMA, 0.0)
            val_a[pl.ds(((i + 1) * COLS + j) * 8, 8), :] = reward

    def take(ref, i):
        return [ref[pl.ds((i * COLS + j) * 8, 8), :] for j in range(COLS)]

    def put(ref, i, vregs):
        for j in range(COLS):
            ref[pl.ds((i * COLS + j) * 8, 8), :] = vregs[j]

    def wrap(ref):
        put(ref, 0, [pltpu.roll(x, 1, 0) for x in take(ref, ROWS)])
        put(ref, ROWS + 1, [pltpu.roll(x, 7, 0) for x in take(ref, 1)])

    def sides_of(now):
        return pltpu.roll(now[COLS - 1], 1, 1), pltpu.roll(now[0], LANES - 1, 1)

    def sweep(source, target):
        above, now = take(source, 0), take(source, 1)
        outer = sides_of(now)
        for i in range(ROWS):
            below = take(source, i + 2)
            left = [outer[0]] + now[:-1]
            right = now[1:] + [outer[1]]
            new = []
            for j in range(COLS):
                best = jnp.maximum(jnp.maximum(above[j], below[j]), jnp.maximum(left[j], right[j]))
                spot = pl.ds((i * COLS + j) * 8, 8)
                new.append(reward_v[spot, :] + decay_v[spot, :] * best)
            put(target, i + 1, new)
            above, now = now, below
            outer = sides_of(now)
        wrap(target)

    wrap(val_a)

    def two_sweeps(index, carry):
        sweep(val_a, val_b)
        sweep(val_b, val_a)
        return carry

    lax.fori_loop(0, SWEEPS // 2, two_sweeps, 0)

    block = jnp.concatenate(
        [
            jnp.concatenate(
                [val_a[pl.ds(((i + 1) * COLS + j) * 8, 8), :] for i in range(ROWS)], axis=0
            )
            for j in range(COLS)
        ],
        axis=1,
    )
    upper = block.astype(BF16)
    lower = (block - upper.astype(F32)).astype(BF16)
    in_lane = iota((WIDE, 4 * TILE), 0)
    spot = iota((WIDE, 4 * TILE), 1)
    column = (in_lane % TASK_LANES) * COLS + in_lane // LANES - HALO
    match = (column == spot % TILE) & (in_lane % LANES // TASK_LANES == spot // TILE)
    back = jnp.where(match, 1.0, 0.0).astype(BF16)
    flat = dot(upper, back) + dot(lower, back)
    for i in range(ROWS):
        for c in range(8):
            piece = flat[8 * i : 8 * i + 8, c * LANES : (c + 1) * LANES]
            natural_v[c, pl.ds(i, 8, stride=ROWS), :] = piece
    stores = []
    for c in range(8):
        stores.append(
            pltpu.make_async_copy(
                natural_v.at[c, pl.ds(HALO, TILE)],
                values_out.at[c // 2, :, pl.ds(c % 2 * LANES, LANES)],
                out_sem.at[c],
            )
        )
        stores[-1].start()

    to_smem.wait()

    def pick(k, carry):
        for a in range(LANES):
            picked_v[pl.ds(k * LANES + a, 1), :] = val_a[pl.ds(index_s[k, a], 1), :]
        return carry

    lax.fori_loop(0, 16, pick, 0)
    square = iota((LANES, LANES), 0)
    diagonal = square == iota((LANES, LANES), 1)
    for k in range(16):
        rows = picked_v[k * LANES : (k + 1) * LANES, :]
        upper = rows.astype(BF16)
        lower = (rows - upper.astype(F32)).astype(BF16)
        select = jnp.where(square == lane_of[:, k * LANES : (k + 1) * LANES], 1.0, 0.0).astype(BF16)
        crossed = dot(upper, select) + dot(lower, select)
        agent_out[:, k * LANES : (k + 1) * LANES] = jnp.sum(
            jnp.where(diagonal, crossed, 0.0), axis=0, keepdims=True
        )
    for store in stores:
        store.wait()


def frame(cells, lists, n, s, w, e, corner, codes, table, task):
    return pl.pallas_call(
        frame_kernel,
        out_shape=(
            jax.ShapeDtypeStruct((4, TILE, TILE), F32),
            jax.ShapeDtypeStruct((1, AGENTS), F32),
        ),
        in_specs=[pl.BlockSpec(memory_space=pltpu.VMEM)] * 10,
        out_specs=[pl.BlockSpec(memory_space=pl.ANY), pl.BlockSpec(memory_space=pltpu.VMEM)],
        scratch_shapes=[
            pltpu.VMEM((3, EXT, LANES), F32),
            pltpu.VMEM((3, EXT, LANES), F32),
            pltpu.VMEM((ROWS * COLS * 8, LANES), F32),
            pltpu.VMEM((ROWS * COLS * 8, LANES), F32),
            pltpu.VMEM(((ROWS + 2) * COLS * 8, LANES), F32),
            pltpu.VMEM(((ROWS + 2) * COLS * 8, LANES), F32),
            pltpu.VMEM((8, EXT, LANES), F32),
            pltpu.VMEM((AGENTS, LANES), F32),
            pltpu.VMEM((16, LANES), I32),
            pltpu.SMEM((16, LANES), I32),
            pltpu.SemaphoreType.DMA((8,)),
            pltpu.SemaphoreType.DMA,
        ],
        compiler_params=pltpu.CompilerParams(vmem_limit_bytes=40 << 20),
        name="frame",
    )(cells, lists, n, s, w, e, corner, codes, table, task)


def on_device(map_codes, reward_table, start_cell, agent_task, actions):
    arrived = exchange(map_codes, start_cell.reshape(1, AGENTS), actions)
    values, agent_value = frame(*arrived, map_codes, reward_table, agent_task.reshape(1, AGENTS))
    return values, agent_value.reshape(AGENTS)


def solution(mesh):
    placed = (P("gy", "gx"), P(), P(("gx", "gy")), P(("gx", "gy")), P(None, ("gx", "gy")))
    return jax.shard_map(
        on_device,
        mesh=mesh,
        in_specs=placed,
        out_specs=(P(None, "gy", "gx"), P(("gx", "gy"))),
        check_vma=False,
    )
```

time: 312 us -> 40.5 us (0.13)
  waiting for transfers between devices: 102 us -> 0 us
  other arithmetic: 75.7 us -> 0 us
  starting transfers between devices: 72.8 us -> 0 us
  local copies, waits for them, and re-layouts: 50.8 us -> 5.96 us
  Pallas kernels: 0 us -> 33.3 us
  matrix products: 6.2 us -> 0 us
    ppermute x32 -> x0, waiting for transfers between devices: 102 us -> none  [the longest x12 65.6 us: with_halo(): lax.ppermute(lax.slice_in_dim(block, block.shape[dim] - width, None, axis...]
    ppermute x32 -> x0, starting transfers between devices: 72.8 us -> none  [the longest x12 46.6 us: with_halo(): lax.ppermute(lax.slice_in_dim(block, 0, width, axis=dim), axis, backward)]
    gather x3 -> x0, local copies, waits for them, and re-layouts: 40.1 us -> none  [the longest x1 17.7 us: on_device(): own_value = flat_values[agent_task, jnp.clip(owner_cell, 0, cell_count - 1)]]
    pallas_call x0 -> x2, Pallas kernels: none -> 33.3 us  [the longest x1 17.3 us: frame(): pl.pallas_call(frame_kernel, out_shape=(jax.ShapeDtypeStruct((4, TILE, TI...]
    add x16 -> x0, other arithmetic: 26 us -> none  [sweep_cells(): return reward + GAMMA * living * highest]
    scatter-add x1 -> x0, other arithmetic: 18.2 us -> none  [on_device(): jnp.zeros((cell_count + 1,), jnp.float32).at[landing].add(1.0)[:cell_count]]
    mul x17 -> x0, other arithmetic: 11.2 us -> none  [the longest x16 11.2 us: sweep_cells(): return reward + GAMMA * living * highest]
    concatenate x9 -> x0, other arithmetic: 9.1 us -> none  [the longest x6 8.29 us: with_halo(): block = jnp.concatenate([low, block, high], axis=dim)]
  transfers between devices with their start and end apart: 32 -> 0, of which waited for: 22 -> 0; matrix products, arithmetic and copies ran while one was open for 18% -> 0% of each run, Pallas kernels for 0% -> 0%
where the time goes in v1:
time: 40.5 us; the launch traced here: 39.9 us
  Pallas kernels  33.3 us (82%)
  local copies, waits for them, and re-layouts  5.96 us (15%)
  between operations  0.68 us (2%)
    pallas_call x1, Pallas kernels, frame(): pl.pallas_call(frame_kernel, out_shape=(jax.ShapeDtypeStruct((4, TILE, TI...  17.3 us
    pallas_call x1, Pallas kernels, exchange(): pl.pallas_call(exchange_kernel, out_shape=(jax.ShapeDtypeStruct((1, AGENT...  16 us
    unnamed x20, local copies, waits for them, and re-layouts  5.96 us

profile of v1, /device:TPU:1, one launch (start us, length us, event | category | flops | bytes accessed | tf_op | source)
XLA Modules:
  0.0 39.9 jit_solution(8546232497882351352)
XLA Ops:
  0.6 0.0 copy-start
  0.6 16.0 %exchange.1 = (s32[1,2048]{1,0:T(1,128)}, s32[8,1,2048]{2,1,0:T(1,128)}, s32[32,256]{1,0:T(8,128)}, s32[32,256]{1,0:T(8,128)}, s32[64,128]{1,0:T(8,128)}, /*index=5*/s32[64,128]{1,0:T(8,128)}, s32[4,8,128]{2,1,0:T(8,128)}) custom-call(s32[1,2048]{1,0:T(1,128)} %bitcast.4, s32[16,2048]{1,0:T(8,128)} %act_hbm.1, s32[256,256]{1,0:T(8,128)} %codes_ref.1), custom_call_target="tpu_custom_call" | custom-call | tf_op jit(solution)/shard_map/exchange/pallas_call | solution.py:139
  16.6 0.0 copy-start.7
  16.6 0.0 copy-start.9
  16.6 0.0 copy-done
  16.6 0.7 %copy-done.7 = s32[2048]{0:T(1024)S(1)} copy-done((s32[2048]{0:T(1024)S(1)}, s32[2048]{0:T(1024)}, u32[]{:S(2)}) %copy-start.7) | copy-done | bytes 8216
  17.3 0.0 copy-done.9
  17.3 0.0 copy-start.1
  17.3 0.8 %copy-done.1 = s32[8,1,2048]{2,1,0:T(1,128)S(1)} copy-done((s32[8,1,2048]{2,1,0:T(1,128)S(1)}, s32[8,1,2048]{2,1,0:T(1,128)}, u32[]{:S(2)}) %copy-start.1) | copy-done | bytes 65560
  18.1 0.0 copy-start.2
  18.1 0.8 %copy-done.2 = s32[32,256]{1,0:T(8,128)S(1)} copy-done((s32[32,256]{1,0:T(8,128)S(1)}, s32[32,256]{1,0:T(8,128)}, u32[]{:S(2)}) %copy-start.2) | copy-done | bytes 32792
  18.9 0.0 copy-start.3
  18.9 0.8 %copy-done.3 = s32[32,256]{1,0:T(8,128)S(1)} copy-done((s32[32,256]{1,0:T(8,128)S(1)}, s32[32,256]{1,0:T(8,128)}, u32[]{:S(2)}) %copy-start.3) | copy-done | bytes 32792
  19.7 0.0 copy-start.4
  19.7 0.8 %copy-done.4 = s32[64,128]{1,0:T(8,128)S(1)} copy-done((s32[64,128]{1,0:T(8,128)S(1)}, s32[64,128]{1,0:T(8,128)}, u32[]{:S(2)}) %copy-start.4) | copy-done | bytes 32792
  20.4 0.0 copy-start.5
  20.4 0.8 %copy-done.5 = s32[64,128]{1,0:T(8,128)S(1)} copy-done((s32[64,128]{1,0:T(8,128)S(1)}, s32[64,128]{1,0:T(8,128)}, u32[]{:S(2)}) %copy-start.5) | copy-done | bytes 32792
  21.2 0.0 copy-start.6
  21.2 0.7 %copy-done.6 = s32[4,8,128]{2,1,0:T(8,128)S(1)} copy-done((s32[4,8,128]{2,1,0:T(8,128)S(1)}, s32[4,8,128]{2,1,0:T(8,128)}, u32[]{:S(2)}) %copy-start.6) | copy-done | bytes 16408
  21.9 0.0 copy-start.8
  21.9 0.7 %copy-done.8 = s32[1,2048]{1,0:T(1,128)S(1)} copy-done((s32[1,2048]{1,0:T(1,128)S(1)}, s32[1,2048]{1,0:T(1,128)}, u32[]{:S(2)}) %copy-start.8) | copy-done | bytes 8216
  22.6 17.3 %frame.1 = (f32[4,256,256]{2,1,0:T(8,128)}, f32[1,2048]{1,0:T(1,128)}) custom-call(s32[1,2048]{1,0:T(1,128)S(1)} %copy-done.8, s32[8,1,2048]{2,1,0:T(1,128)S(1)} %copy-done.1, s32[32,256]{1,0:T(8,128)S(1)} %copy-done.2, s32[32,256]{1,0:T(8,128)S(1)} %copy-done.3, s32[64,128]{1,0:T(8,128)S(1)} %copy-done.4, s32[64,128]{1,0:T(8,128)S(1)} %copy-done.5, ...), custom_call_target="tpu_custom_call" | custom-call | tf_op jit(solution)/shard_map/frame/pallas_call | solution.py:383
Async XLA Ops:
  0.6 16.0 %copy-start = (s32[256,256]{1,0:T(8,128)S(1)}, s32[256,256]{1,0:T(8,128)}, u32[]{:S(2)}) copy-start(s32[256,256]{1,0:T(8,128)} %codes_ref.1) | copy-start | bytes 786436
  16.6 0.7 %copy-start.7 = (s32[2048]{0:T(1024)S(1)}, s32[2048]{0:T(1024)}, u32[]{:S(2)}) copy-start(s32[2048]{0:T(1024)} %param.8) | copy-start | bytes 24580
  16.6 0.7 %copy-start.9 = (f32[4,64]{1,0:T(4,128)S(1)}, f32[4,64]{1,0:T(4,128)}, u32[]{:S(2)}) copy-start(f32[4,64]{1,0:T(4,128)} %table_ref.1) | copy-start | bytes 3076
  17.3 0.8 %copy-start.1 = (s32[8,1,2048]{2,1,0:T(1,128)S(1)}, s32[8,1,2048]{2,1,0:T(1,128)}, u32[]{:S(2)}) copy-start(s32[8,1,2048]{2,1,0:T(1,128)} %get-tuple-element.12.lists_ref) | copy-start | bytes 196612
  18.1 0.8 %copy-start.2 = (s32[32,256]{1,0:T(8,128)S(1)}, s32[32,256]{1,0:T(8,128)}, u32[]{:S(2)}) copy-start(s32[32,256]{1,0:T(8,128)} %get-tuple-element.13.n_ref) | copy-start | bytes 98308
  18.9 0.8 %copy-start.3 = (s32[32,256]{1,0:T(8,128)S(1)}, s32[32,256]{1,0:T(8,128)}, u32[]{:S(2)}) copy-start(s32[32,256]{1,0:T(8,128)} %get-tuple-element.14.s_ref) | copy-start | bytes 98308
  19.7 0.8 %copy-start.4 = (s32[64,128]{1,0:T(8,128)S(1)}, s32[64,128]{1,0:T(8,128)}, u32[]{:S(2)}) copy-start(s32[64,128]{1,0:T(8,128)} %get-tuple-element.15.w_ref) | copy-start | bytes 98308
  20.4 0.8 %copy-start.5 = (s32[64,128]{1,0:T(8,128)S(1)}, s32[64,128]{1,0:T(8,128)}, u32[]{:S(2)}) copy-start(s32[64,128]{1,0:T(8,128)} %get-tuple-element.16.e_ref) | copy-start | bytes 98308
  21.2 0.7 %copy-start.6 = (s32[4,8,128]{2,1,0:T(8,128)S(1)}, s32[4,8,128]{2,1,0:T(8,128)}, u32[]{:S(2)}) copy-start(s32[4,8,128]{2,1,0:T(8,128)} %get-tuple-element.17.corner_ref) | copy-start | bytes 49156
  21.9 0.7 %copy-start.8 = (s32[1,2048]{1,0:T(1,128)S(1)}, s32[1,2048]{1,0:T(1,128)}, u32[]{:S(2)}) copy-start(s32[1,2048]{1,0:T(1,128)} %get-tuple-element.11.cells_ref) | copy-start | bytes 24580

commit v2 on v1

v2 whole, which is shorter than its diff:
```python
import functools

import jax
import jax.numpy as jnp
from jax import lax
from jax.experimental import pallas as pl
from jax.experimental.pallas import tpu as pltpu
from jax.sharding import PartitionSpec as P

SWEEPS = 16
CODES = 64
TERMINAL = 2
GAMMA = 0.95
PENALTY = 0.5
CORNERS = ((-1, -1), (-1, 1), (1, -1), (1, 1))
SIDES = ((-1, 0), (0, -1), (0, 1), (1, 0))
NEIGHBOURS = ((-1, -1), (-1, 0), (-1, 1), (0, -1), (0, 1), (1, -1), (1, 0), (1, 1))

TILE = 256
HALO = 32
EXT = TILE + 2 * HALO
ROWS = EXT // 8
COLS = 10
LANES = 128
TASK_LANES = 32
WIDE = COLS * LANES
AGENTS = 2048
STRIDE = 512
EDGE = 48
FAR = EXT - EDGE

F32 = jnp.float32
BF16 = jnp.bfloat16
F8 = jnp.float8_e4m3fn
I32 = jnp.int32
MESH = pl.DeviceIdType.MESH
NT = (((1,), (1,)), ((), ()))
NN = (((1,), (0,)), ((), ()))


def dot(a, b, dims=NN):
    return lax.dot_general(a, b, dims, preferred_element_type=F32)


def iota(shape, dim):
    return lax.broadcasted_iota(I32, shape, dim)


def one(match, kind):
    return jnp.where(match, 1.0, 0.0).astype(kind)


def hot(values, count):
    return one(iota((count, values.shape[1]), 0) == values, F8)


def slots(cols, low, high):
    near = (cols >= low) & (cols < low + EDGE)
    far = (cols >= high) & (cols < high + EDGE)
    return jnp.where(near, cols - low, jnp.where(far, cols - high + 64, -1))


def inner_slots(cols):
    return jnp.where((cols >= EDGE) & (cols < FAR), cols - EDGE, -1)


def exchange_kernel(
    start_hbm, act_hbm, codes_hbm, task_hbm,
    lists_out, n_out, s_out, w_out, e_out, corner_out, codes_out, count_out,
    spread_codes, spread_counts, back_out, index_out, select_out,
    start_v, act_v, task_v, cells_v, w_send, e_send, corner_send, local_sem, send_sem, recv_sem,
):
    gx = lax.axis_index("gx")
    gy = lax.axis_index("gy")

    def device(step):
        return (lax.rem(gx + step[1] + 16, 16), lax.rem(gy + step[0] + 16, 16))

    loads = [
        pltpu.make_async_copy(act_hbm, act_v, local_sem.at[0]),
        pltpu.make_async_copy(start_hbm, start_v, local_sem.at[1]),
        pltpu.make_async_copy(codes_hbm, codes_out, local_sem.at[2]),
        pltpu.make_async_copy(task_hbm, task_v, local_sem.at[3]),
    ]
    for load in loads:
        load.start()
    barrier = pltpu.get_barrier_semaphore()
    for step in NEIGHBOURS:
        pl.semaphore_signal(barrier, inc=1, device_id=device(step), device_id_type=MESH)

    loads[0].wait()
    loads[1].wait()
    act = act_v[...]
    start = start_v[...]
    row = (start >> 8) + HALO
    col = (start & 255) + HALO
    row += jnp.sum((act == 2).astype(I32) - (act == 1).astype(I32), axis=0, keepdims=True)
    col += jnp.sum((act == 4).astype(I32) - (act == 3).astype(I32), axis=0, keepdims=True)
    cells_v[...] = row * STRIDE + col

    targets = [hot(inner_slots(col), 256), hot(slots(col, 0, FAR), 128), hot(slots(col, 16, 256), 128)]
    own = dot(hot(row, EXT), jnp.concatenate(targets, axis=0), NT)
    for c in range(3):
        count_out[c] = own[:, c * LANES : (c + 1) * LANES]

    loads[2].wait()
    lane = iota((64, LANES), 1)
    west = jnp.zeros((64, LANES), I32)
    east = jnp.zeros((64, LANES), I32)
    for q in range(4):
        mine = (lane >= 32 * q) & (lane < 32 * q + 32)
        rows = pl.ds(64 * q, 64)
        west = jnp.where(mine, pltpu.roll(codes_out[rows, 0:128], 32 * q, 1), west)
        east = jnp.where(mine, pltpu.roll(codes_out[rows, 128:256], (32 * q + 32) % 128, 1), east)
    w_send[...] = west
    e_send[...] = east
    lane8 = iota((8, LANES), 1)
    lane24 = iota((24, LANES), 1)
    for k, (r, c) in enumerate(CORNERS):
        piece = jnp.zeros((8, LANES), I32)
        for q in range(4):
            mine = (lane8 >= 32 * q) & (lane8 < 32 * q + 32)
            rows = pl.ds((0 if r < 0 else 224) + 8 * q, 8)
            if c < 0:
                part = pltpu.roll(codes_out[rows, 0:128], 32 * q, 1)
            else:
                part = pltpu.roll(codes_out[rows, 128:256], (32 * q + 32) % 128, 1)
            piece = jnp.where(mine, part, piece)
        corner_send[k, 0:8, :] = piece
        first = 16 if r < 0 else 256
        upper = own[first : first + 24, 384:512]
        lower = own[first + 24 : first + 48, 384:512]
        if c < 0:
            lower = pltpu.roll(lower, 64, 1)
        else:
            upper = pltpu.roll(upper, 64, 1)
        corner_send[k, 8:32, :] = jnp.where(lane24 < 64, upper, lower).astype(I32)

    pl.semaphore_wait(barrier, 8)
    copies = []

    def send(source, target, step):
        k = len(copies)
        copy = pltpu.make_async_remote_copy(
            source, target, send_sem.at[k], recv_sem.at[k],
            device_id=device(step), device_id_type=MESH,
        )
        copy.start()
        copies.append(copy)

    send(w_send, e_out, (0, -1))
    send(e_send, w_out, (0, 1))
    for k, step in enumerate(CORNERS):
        send(corner_send.at[k], corner_out.at[3 - k], step)
    for k in (1, 2, 0, 3):
        send(cells_v, lists_out.at[3 - k], SIDES[k])
    send(codes_out.at[pl.ds(0, 32)], s_out, (-1, 0))
    send(codes_out.at[pl.ds(224, 32)], n_out, (1, 0))

    loads[3].wait()
    block = (row * 1639) >> 16
    group = (col * 6554) >> 16
    place = ((row - block * ROWS + 1) * COLS + (col - group * COLS)) * 8 + block
    lane_of = task_v[...] * TASK_LANES + group
    for k in range(16):
        part = slice(k * LANES, (k + 1) * LANES)
        index_out[k : k + 1, :] = place[:, part]
        select_out[:, part] = one(iota((LANES, LANES), 0) == lane_of[:, part], BF16)

    slot = iota((384, LANES), 0)
    code_col = jnp.where(slot < 256, slot + HALO, jnp.where(slot < 288, slot - 256, slot))
    code_col = jnp.where(slot < 320, code_col, -1)
    count_col = jnp.where(slot < FAR - EDGE, slot + EDGE, -1)
    count_col = jnp.where((slot >= 256) & (slot < 256 + EDGE), slot - 256, count_col)
    count_col = jnp.where((slot >= 320) & (slot < 320 + EDGE), slot - 320 + FAR, count_col)
    first_col = (iota((1, LANES), 1) & 31) * COLS
    in_lane = iota((LANES, LANES), 0)
    to_lane = iota((LANES, LANES), 1)
    for j in range(COLS):
        part = slice(j * LANES, (j + 1) * LANES)
        spread_codes[:, part] = one(code_col == first_col + j, BF16)
        spread_counts[:, part] = one(count_col == first_col + j, BF16)
        column = (in_lane & 31) * COLS + (j - HALO)
        column = jnp.where((column >= 0) & (column < TILE), column + (in_lane >> 5) * TILE, -1)
        for k in range(8):
            back_out[part, k * LANES : (k + 1) * LANES] = one(column == to_lane + k * LANES, BF16)
    for copy in copies:
        copy.wait()


def exchange(codes, start, actions, task):
    return pl.pallas_call(
        exchange_kernel,
        out_shape=(
            pltpu.VMEM((4, 1, AGENTS), I32),
            pltpu.VMEM((32, TILE), I32),
            pltpu.VMEM((32, TILE), I32),
            pltpu.VMEM((64, LANES), I32),
            pltpu.VMEM((64, LANES), I32),
            pltpu.VMEM((4, 32, LANES), I32),
            pltpu.VMEM((TILE, TILE), I32),
            pltpu.VMEM((3, EXT, LANES), F32),
            pltpu.VMEM((384, WIDE), BF16),
            pltpu.VMEM((384, WIDE), BF16),
            pltpu.VMEM((WIDE, 4 * TILE), BF16),
            pltpu.VMEM((16, LANES), I32),
            pltpu.VMEM((LANES, AGENTS), BF16),
        ),
        in_specs=[pl.BlockSpec(memory_space=pltpu.HBM)] * 4,
        out_specs=[pl.BlockSpec(memory_space=pltpu.VMEM)] * 13,
        scratch_shapes=[
            pltpu.VMEM((1, AGENTS), I32),
            pltpu.VMEM((16, AGENTS), I32),
            pltpu.VMEM((1, AGENTS), I32),
            pltpu.VMEM((1, AGENTS), I32),
            pltpu.VMEM((64, LANES), I32),
            pltpu.VMEM((64, LANES), I32),
            pltpu.VMEM((4, 32, LANES), I32),
            pltpu.SemaphoreType.DMA((4,)),
            pltpu.SemaphoreType.DMA((12,)),
            pltpu.SemaphoreType.DMA((12,)),
        ],
        compiler_params=pltpu.CompilerParams(
            collective_id=0, has_side_effects=True, vmem_limit_bytes=24 << 20
        ),
        name="exchange",
    )(start, actions, codes, task)


def frame_kernel(
    lists_ref, n_ref, s_ref, w_ref, e_ref, corner_ref, codes_ref, own_ref,
    spread_codes, spread_counts, back_ref, index_v, select_ref, table_hbm,
    values_out, agent_out,
    codes_v, count_v, reward_v, decay_v, val_a, val_b, natural_v, picked_v,
    index_s, table_ref, out_sem, index_sem, table_sem,
):
    to_smem = pltpu.make_async_copy(index_v, index_s, index_sem)
    to_smem.start()
    to_table = pltpu.make_async_copy(table_hbm, table_ref, table_sem)
    to_table.start()

    def cells_of(k):
        cells = lists_ref[k]
        step = SIDES[k]
        return (cells >> 9) + step[0] * TILE, (cells & (STRIDE - 1)) + step[1] * TILE

    row, col = cells_of(1)
    edges = own_ref[2] + dot(hot(row, EXT), hot(slots(col, 0, FAR), 128), NT)
    row, col = cells_of(2)
    count_v[2] = edges + dot(hot(row, EXT), hot(slots(col, 0, FAR), 128), NT)
    count_v[0] = own_ref[0]
    count_v[1] = own_ref[1]
    lane24 = iota((24, LANES), 1)
    for k, first, pair in ((0, 0, 0), (3, FAR, 2)):
        row, col = cells_of(k)
        targets = [hot(inner_slots(col), 256), hot(slots(col, 0, FAR), 128)]
        part = dot(hot(row - first, EDGE), jnp.concatenate(targets, axis=0), NT)
        band = slice(first, first + EDGE)
        for c in range(3):
            count_v[c, band, :] += part[:, c * LANES : (c + 1) * LANES]
        west = corner_ref[pair, 8:32, :].astype(F32)
        east = corner_ref[pair + 1, 8:32, :].astype(F32)
        west2 = pltpu.roll(west, 64, 1)
        east2 = pltpu.roll(east, 64, 1)
        count_v[2, first : first + 24, :] += jnp.where(lane24 < 64, west, east2)
        count_v[2, first + 24 : first + 48, :] += jnp.where(lane24 < 64, west2, east)

    for c in range(2):
        part = pl.ds(c * LANES, LANES)
        codes_v[c, 0:32, :] = n_ref[:, part].astype(F32)
        codes_v[c, 32:288, :] = codes_ref[:, part].astype(F32)
        codes_v[c, 288:320, :] = s_ref[:, part].astype(F32)
    lane = iota((64, LANES), 1)
    for q in range(4):
        west = pltpu.roll(w_ref[...], (128 - 32 * q) % 128, 1)
        east = pltpu.roll(e_ref[...], (160 - 32 * q) % 128, 1)
        both = jnp.where(lane < 32, west, jnp.where(lane < 64, east, 0))
        codes_v[2, 32 + 64 * q : 96 + 64 * q, :] = both.astype(F32)
        for first, pair in ((0, 0), (288, 2)):
            west = pltpu.roll(corner_ref[pair, 0:8, :], (128 - 32 * q) % 128, 1)
            east = pltpu.roll(corner_ref[pair + 1, 0:8, :], (160 - 32 * q) % 128, 1)
            both = jnp.where(lane[0:8] < 32, west, jnp.where(lane[0:8] < 64, east, 0))
            codes_v[2, first + 8 * q : first + 8 * q + 8, :] = both.astype(F32)

    def interleaved(ref):
        return jnp.concatenate(
            [
                jnp.concatenate([ref[c, pl.ds(i, 8, stride=ROWS), :] for i in range(ROWS)], axis=0)
                for c in range(3)
            ],
            axis=1,
        )

    counts = interleaved(count_v)
    high = jnp.floor(counts * (1.0 / 128.0))
    low = counts - high * 128.0
    minus = dot((high * (-128.0 * PENALTY)).astype(BF16), spread_counts[...])
    minus += dot((low * -PENALTY).astype(BF16), spread_counts[...])
    wide = dot(interleaved(codes_v).astype(BF16), spread_codes[...])

    to_table.wait()
    lane8 = iota((8, LANES), 1)
    table = []
    for k in range(2):
        pair = jnp.concatenate([table_ref[2 * k : 2 * k + 1, :], table_ref[2 * k + 1 : 2 * k + 2, :]], axis=1)
        table.append(jnp.broadcast_to(pair, (8, LANES)))
    shift = (lane8 // TASK_LANES % 2) * CODES
    for i in range(ROWS):
        for j in range(COLS):
            code = wide[8 * i : 8 * i + 8, LANES * j : LANES * (j + 1)].astype(I32)
            at = code + shift
            found = jnp.where(
                lane8 < 64,
                jnp.take_along_axis(table[0], at, axis=1),
                jnp.take_along_axis(table[1], at, axis=1),
            )
            reward = found + minus[8 * i : 8 * i + 8, LANES * j : LANES * (j + 1)]
            spot = pl.ds((i * COLS + j) * 8, 8)
            reward_v[spot, :] = reward
            decay_v[spot, :] = jnp.where(code < CODES - TERMINAL, GAMMA, 0.0)
            val_a[pl.ds(((i + 1) * COLS + j) * 8, 8), :] = reward

    def take(ref, i):
        return [ref[pl.ds((i * COLS + j) * 8, 8), :] for j in range(COLS)]

    def put(ref, i, vregs):
        for j in range(COLS):
            ref[pl.ds((i * COLS + j) * 8, 8), :] = vregs[j]

    def wrap(ref):
        put(ref, 0, [pltpu.roll(x, 1, 0) for x in take(ref, ROWS)])
        put(ref, ROWS + 1, [pltpu.roll(x, 7, 0) for x in take(ref, 1)])

    def sides_of(now):
        return pltpu.roll(now[COLS - 1], 1, 1), pltpu.roll(now[0], LANES - 1, 1)

    def sweep(source, target):
        above, now = take(source, 0), take(source, 1)
        outer = sides_of(now)
        for i in range(ROWS):
            below = take(source, i + 2)
            left = [outer[0]] + now[:-1]
            right = now[1:] + [outer[1]]
            new = []
            for j in range(COLS):
                best = jnp.maximum(jnp.maximum(above[j], below[j]), jnp.maximum(left[j], right[j]))
                spot = pl.ds((i * COLS + j) * 8, 8)
                new.append(reward_v[spot, :] + decay_v[spot, :] * best)
            put(target, i + 1, new)
            above, now = now, below
            outer = sides_of(now)
        wrap(target)

    wrap(val_a)

    def two_sweeps(index, carry):
        sweep(val_a, val_b)
        sweep(val_b, val_a)
        return carry

    lax.fori_loop(0, SWEEPS // 2, two_sweeps, 0)

    block = jnp.concatenate(
        [
            jnp.concatenate(
                [val_a[pl.ds(((i + 1) * COLS + j) * 8, 8), :] for i in range(ROWS)], axis=0
            )
            for j in range(COLS)
        ],
        axis=1,
    )
    upper = block.astype(BF16)
    lower = (block - upper.astype(F32)).astype(BF16)
    back = back_ref[...]
    flat = dot(upper, back) + dot(lower, back)
    for i in range(ROWS):
        for c in range(8):
            piece = flat[8 * i : 8 * i + 8, c * LANES : (c + 1) * LANES]
            natural_v[c, pl.ds(i, 8, stride=ROWS), :] = piece
    stores = []
    for c in range(8):
        stores.append(
            pltpu.make_async_copy(
                natural_v.at[c, pl.ds(HALO, TILE)],
                values_out.at[c // 2, :, pl.ds(c % 2 * LANES, LANES)],
                out_sem.at[c],
            )
        )
        stores[-1].start()

    to_smem.wait()

    def pick(k, carry):
        for a in range(LANES):
            picked_v[pl.ds(k * LANES + a, 1), :] = val_a[pl.ds(index_s[k, a], 1), :]
        return carry

    lax.fori_loop(0, 16, pick, 0)
    diagonal = iota((LANES, LANES), 0) == iota((LANES, LANES), 1)
    for k in range(16):
        rows = picked_v[k * LANES : (k + 1) * LANES, :]
        upper = rows.astype(BF16)
        lower = (rows - upper.astype(F32)).astype(BF16)
        select = select_ref[:, k * LANES : (k + 1) * LANES]
        crossed = dot(upper, select) + dot(lower, select)
        agent_out[:, k * LANES : (k + 1) * LANES] = jnp.sum(
            jnp.where(diagonal, crossed, 0.0), axis=0, keepdims=True
        )
    for store in stores:
        store.wait()


def frame(*arrays):
    return pl.pallas_call(
        frame_kernel,
        out_shape=(
            jax.ShapeDtypeStruct((4, TILE, TILE), F32),
            jax.ShapeDtypeStruct((1, AGENTS), F32),
        ),
        in_specs=[pl.BlockSpec(memory_space=pltpu.VMEM)] * 13 + [pl.BlockSpec(memory_space=pltpu.HBM)],
        out_specs=[pl.BlockSpec(memory_space=pltpu.HBM), pl.BlockSpec(memory_space=pltpu.VMEM)],
        scratch_shapes=[
            pltpu.VMEM((3, EXT, LANES), F32),
            pltpu.VMEM((3, EXT, LANES), F32),
            pltpu.VMEM((ROWS * COLS * 8, LANES), F32),
            pltpu.VMEM((ROWS * COLS * 8, LANES), F32),
            pltpu.VMEM(((ROWS + 2) * COLS * 8, LANES), F32),
            pltpu.VMEM(((ROWS + 2) * COLS * 8, LANES), F32),
            pltpu.VMEM((8, EXT, LANES), F32),
            pltpu.VMEM((AGENTS, LANES), F32),
            pltpu.SMEM((16, LANES), I32),
            pltpu.VMEM((4, CODES), F32),
            pltpu.SemaphoreType.DMA((8,)),
            pltpu.SemaphoreType.DMA,
            pltpu.SemaphoreType.DMA,
        ],
        compiler_params=pltpu.CompilerParams(vmem_limit_bytes=40 << 20),
        name="frame",
    )(*arrays)


def on_device(map_codes, reward_table, start_cell, agent_task, actions):
    arrived = exchange(
        map_codes, start_cell.reshape(1, AGENTS), actions, agent_task.reshape(1, AGENTS)
    )
    values, agent_value = frame(*arrived, reward_table)
    return values, agent_value.reshape(AGENTS)


def solution(mesh):
    placed = (P("gy", "gx"), P(), P(("gx", "gy")), P(("gx", "gy")), P(None, ("gx", "gy")))
    return jax.shard_map(
        on_device,
        mesh=mesh,
        in_specs=placed,
        out_specs=(P(None, "gy", "gx"), P(("gx", "gy"))),
        check_vma=False,
    )
```

time: 40.5 us -> 35.9 us (0.89)
  Pallas kernels: 33.3 us -> 31.1 us
  local copies, waits for them, and re-layouts: 5.96 us -> 3.92 us
    unnamed x20 -> x10, local copies, waits for them, and re-layouts: 5.96 us -> 3.92 us
    pallas_call x1, Pallas kernels: 17.3 us -> 15.8 us  [frame(): pl.pallas_call(frame_kernel, out_shape=(jax.ShapeDtypeStruct((4, TILE, TI...]
    pallas_call x1, Pallas kernels: 16 us -> 15.3 us  [exchange(): pl.pallas_call(exchange_kernel, out_shape=(pltpu.VMEM((4, 1, AGENTS), I32...]
where the time goes in v2:
time: 35.9 us; the launch traced here: 35.6 us
  Pallas kernels  31.1 us (87%)
  local copies, waits for them, and re-layouts  3.92 us (11%)
  between operations  0.66 us (2%)
    pallas_call x1, Pallas kernels, frame(): pl.pallas_call(frame_kernel, out_shape=(jax.ShapeDtypeStruct((4, TILE, TI...  15.8 us
    pallas_call x1, Pallas kernels, exchange(): pl.pallas_call(exchange_kernel, out_shape=(pltpu.VMEM((4, 1, AGENTS), I32...  15.3 us
    unnamed x10, local copies, waits for them, and re-layouts  3.92 us

profile of v2, /device:TPU:1, one launch (start us, length us, event | category | flops | bytes accessed | tf_op | source)
XLA Modules:
  0.0 35.6 jit_solution(2339490152540200216)
XLA Ops:
  0.6 0.0 copy-start
  0.6 0.9 %copy-done = s32[256,256]{1,0:T(8,128)S(1)} copy-done((s32[256,256]{1,0:T(8,128)S(1)}, s32[256,256]{1,0:T(8,128)}, u32[]{:S(2)}) %copy-start) | copy-done | bytes 262168
  1.6 0.0 copy-start.1
  1.6 0.9 %copy-done.1 = s32[16,2048]{1,0:T(8,128)S(1)} copy-done((s32[16,2048]{1,0:T(8,128)S(1)}, s32[16,2048]{1,0:T(8,128)}, u32[]{:S(2)}) %copy-start.1) | copy-done | bytes 131096
  2.5 0.0 copy-start.2
  2.5 0.7 %copy-done.2 = s32[2048]{0:T(1024)S(1)} copy-done((s32[2048]{0:T(1024)S(1)}, s32[2048]{0:T(1024)}, u32[]{:S(2)}) %copy-start.2) | copy-done | bytes 8216
  3.2 0.0 copy-start.3
  3.2 0.7 %copy-done.3 = s32[2048]{0:T(1024)S(1)} copy-done((s32[2048]{0:T(1024)S(1)}, s32[2048]{0:T(1024)}, u32[]{:S(2)}) %copy-start.3) | copy-done | bytes 8216
  3.9 15.3 %exchange.1 = (s32[4,1,2048]{2,1,0:T(1,128)S(1)}, s32[32,256]{1,0:T(8,128)S(1)}, s32[32,256]{1,0:T(8,128)S(1)}, s32[64,128]{1,0:T(8,128)S(1)}, s32[64,128]{1,0:T...) custom-call(s32[1,2048]{1,0:T(1,128)S(1)} %bitcast.3, ...), custom_call_target="tpu_custom_call" | custom-call | tf_op jit(solution)/shard_map/exchange/pallas_call | solution.py:192
  19.1 0.0 copy-start.4
  19.2 0.7 %copy-done.4 = f32[4,64]{1,0:T(4,128)S(1)} copy-done((f32[4,64]{1,0:T(4,128)S(1)}, f32[4,64]{1,0:T(4,128)}, u32[]{:S(2)}) %copy-start.4) | copy-done | bytes 1048
  19.8 15.8 %frame.1 = (f32[4,256,256]{2,1,0:T(8,128)}, f32[1,2048]{1,0:T(1,128)}) custom-call(s32[4,1,2048]{2,1,0:T(1,128)S(1)} %get-tuple-element.17.lists_ref, s32[32,256]{1,0:T(8,128)S(1)} %get-tuple-element.18.n_ref, s32[32,256]{1,0:T(8,128)S(1)} %get-tuple-element.19.s_ref, s32[64,128]{1,0:T(8,128)S(1)} %get-tuple-element.20.w_ref, ...), custom_call_target="tpu_custom_call" | custom-call | tf_op jit(solution)/shard_map/frame/pallas_call | solution.py:414
Async XLA Ops:
  0.6 1.0 %copy-start = (s32[256,256]{1,0:T(8,128)S(1)}, s32[256,256]{1,0:T(8,128)}, u32[]{:S(2)}) copy-start(s32[256,256]{1,0:T(8,128)} %codes_hbm.1) | copy-start | bytes 786436
  1.6 0.9 %copy-start.1 = (s32[16,2048]{1,0:T(8,128)S(1)}, s32[16,2048]{1,0:T(8,128)}, u32[]{:S(2)}) copy-start(s32[16,2048]{1,0:T(8,128)} %act_hbm.1) | copy-start | bytes 393220
  2.5 0.7 %copy-start.2 = (s32[2048]{0:T(1024)S(1)}, s32[2048]{0:T(1024)}, u32[]{:S(2)}) copy-start(s32[2048]{0:T(1024)} %param.7) | copy-start | bytes 24580
  3.2 0.7 %copy-start.3 = (s32[2048]{0:T(1024)S(1)}, s32[2048]{0:T(1024)}, u32[]{:S(2)}) copy-start(s32[2048]{0:T(1024)} %param.8) | copy-start | bytes 24580
  19.1 0.7 %copy-start.4 = (f32[4,64]{1,0:T(4,128)S(1)}, f32[4,64]{1,0:T(4,128)}, u32[]{:S(2)}) copy-start(f32[4,64]{1,0:T(4,128)} %table_hbm.1) | copy-start | bytes 3076

commit v3 on v2

--- a/solution.py
+++ b/solution.py
@@ -224,7 +224,7 @@
             collective_id=0, has_side_effects=True, vmem_limit_bytes=24 << 20
         ),
         name="exchange",
-    )(start, actions, codes, task)
+    )(*[pltpu.with_memory_space_constraint(x, pltpu.HBM) for x in (start, actions, codes, task)])
 
 
 def frame_kernel(
@@ -443,7 +443,7 @@
     arrived = exchange(
         map_codes, start_cell.reshape(1, AGENTS), actions, agent_task.reshape(1, AGENTS)
     )
-    values, agent_value = frame(*arrived, reward_table)
+    values, agent_value = frame(*arrived, pltpu.with_memory_space_constraint(reward_table, pltpu.HBM))
     return values, agent_value.reshape(AGENTS)
 
 

time: 35.9 us -> 31.8 us (0.89)
  local copies, waits for them, and re-layouts: 3.92 us -> 0 us
    unnamed x10 -> x0, local copies, waits for them, and re-layouts: 3.92 us -> none
where the time goes in v3:
time: 31.8 us; the launch traced here: 31.7 us
  Pallas kernels  31 us (97%)
  between operations  0.64 us (2%)
    pallas_call x1, Pallas kernels, frame(): pl.pallas_call(frame_kernel, out_shape=(jax.ShapeDtypeStruct((4, TILE, TI...  15.8 us
    pallas_call x1, Pallas kernels, exchange(): pl.pallas_call(exchange_kernel, out_shape=(pltpu.VMEM((4, 1, AGENTS), I32...  15.2 us

profile of v3, /device:TPU:1, one launch (start us, length us, event | category | flops | bytes accessed | tf_op | source)
XLA Modules:
  0.0 31.7 jit_solution(7838010509144863027)
XLA Ops:
  0.6 15.2 %exchange.1 = (s32[4,1,2048]{2,1,0:T(1,128)S(1)}, s32[32,256]{1,0:T(8,128)S(1)}, s32[32,256]{1,0:T(8,128)S(1)}, s32[64,128]{1,0:T(8,128)S(1)}, s32[64,128]{1,0:T...) custom-call(s32[1,2048]{1,0:T(1,128)} %bitcast.3, ...), custom_call_target="tpu_custom_call" | custom-call | tf_op jit(solution)/shard_map/exchange/pallas_call | solution.py:192
  15.9 15.8 %frame.1 = (f32[4,256,256]{2,1,0:T(8,128)}, f32[1,2048]{1,0:T(1,128)}) custom-call(s32[4,1,2048]{2,1,0:T(1,128)S(1)} %get-tuple-element.17.lists_ref, s32[32,256]{1,0:T(8,128)S(1)} %get-tuple-element.18.n_ref, s32[32,256]{1,0:T(8,128)S(1)} %get-tuple-element.19.s_ref, s32[64,128]{1,0:T(8,128)S(1)} %get-tuple-element.20.w_ref, ...), custom_call_target="tpu_custom_call" | custom-call | tf_op jit(solution)/shard_map/frame/pallas_call | solution.py:414

commit v4 on v3

--- a/solution.py
+++ b/solution.py
@@ -64,11 +64,25 @@
     return jnp.where((cols >= EDGE) & (cols < FAR), cols - EDGE, -1)
 
 
+def interleaved(ref, tiles):
+    parts = []
+    for c in range(tiles):
+        rows = [ref[c, pl.ds(i, 8, stride=ROWS), :] for i in range(ROWS)]
+        parts.append(jnp.concatenate(rows, axis=0))
+    return jnp.concatenate(parts, axis=1)
+
+
+def limbs(counts):
+    high = jnp.floor(counts * (1.0 / 128.0))
+    low = counts - high * 128.0
+    return (high * (-128.0 * PENALTY)).astype(BF16), (low * -PENALTY).astype(BF16)
+
+
 def exchange_kernel(
     start_hbm, act_hbm, codes_hbm, task_hbm,
-    lists_out, n_out, s_out, w_out, e_out, corner_out, codes_out, count_out,
+    side_out, w_out, e_out, corner_out, edge_out, code_out, minus_out,
     spread_codes, spread_counts, back_out, index_out, select_out,
-    start_v, act_v, task_v, cells_v, w_send, e_send, corner_send, local_sem, send_sem, recv_sem,
+    lists_v, n_v, s_v, codes_v, count_v, wide_v, start_v, act_v, task_v, cells_v, w_send, e_send, corner_send, local_sem, send_sem, recv_sem,
 ):
     gx = lax.axis_index("gx")
     gy = lax.axis_index("gy")
@@ -79,7 +93,7 @@
     loads = [
         pltpu.make_async_copy(act_hbm, act_v, local_sem.at[0]),
         pltpu.make_async_copy(start_hbm, start_v, local_sem.at[1]),
-        pltpu.make_async_copy(codes_hbm, codes_out, local_sem.at[2]),
+        pltpu.make_async_copy(codes_hbm, codes_v, local_sem.at[2]),
         pltpu.make_async_copy(task_hbm, task_v, local_sem.at[3]),
     ]
     for load in loads:
@@ -98,11 +112,6 @@
     col += jnp.sum((act == 4).astype(I32) - (act == 3).astype(I32), axis=0, keepdims=True)
     cells_v[...] = row * STRIDE + col
 
-    targets = [hot(inner_slots(col), 256), hot(slots(col, 0, FAR), 128), hot(slots(col, 16, 256), 128)]
-    own = dot(hot(row, EXT), jnp.concatenate(targets, axis=0), NT)
-    for c in range(3):
-        count_out[c] = own[:, c * LANES : (c + 1) * LANES]
-
     loads[2].wait()
     lane = iota((64, LANES), 1)
     west = jnp.zeros((64, LANES), I32)
@@ -110,10 +119,37 @@
     for q in range(4):
         mine = (lane >= 32 * q) & (lane < 32 * q + 32)
         rows = pl.ds(64 * q, 64)
-        west = jnp.where(mine, pltpu.roll(codes_out[rows, 0:128], 32 * q, 1), west)
-        east = jnp.where(mine, pltpu.roll(codes_out[rows, 128:256], (32 * q + 32) % 128, 1), east)
+        west = jnp.where(mine, pltpu.roll(codes_v[rows, 0:128], 32 * q, 1), west)
+        east = jnp.where(mine, pltpu.roll(codes_v[rows, 128:256], (32 * q + 32) % 128, 1), east)
     w_send[...] = west
     e_send[...] = east
+    pl.semaphore_wait(barrier, 8)
+    copies = []
+
+    def send(source, target, step):
+        k = len(copies)
+        copy = pltpu.make_async_remote_copy(
+            source, target, send_sem.at[k], recv_sem.at[k],
+            device_id=device(step), device_id_type=MESH,
+        )
+        copy.start()
+        copies.append(copy)
+
+    send(cells_v, side_out.at[1], (0, -1))
+    send(cells_v, side_out.at[0], (0, 1))
+    send(w_send, e_out, (0, -1))
+    send(e_send, w_out, (0, 1))
+    send(cells_v, lists_v.at[1], (-1, 0))
+    send(cells_v, lists_v.at[0], (1, 0))
+    send(codes_v.at[pl.ds(0, 32)], s_v, (-1, 0))
+    send(codes_v.at[pl.ds(224, 32)], n_v, (1, 0))
+
+    targets = [hot(inner_slots(col), 256), hot(slots(col, 0, FAR), 128), hot(slots(col, 16, 256), 128)]
+    own = dot(hot(row, EXT), jnp.concatenate(targets, axis=0), NT)
+    for c in range(2):
+        count_v[c] = own[:, c * LANES : (c + 1) * LANES]
+    edge_out[...] = own[:, 256:384]
+
     lane8 = iota((8, LANES), 1)
     lane24 = iota((24, LANES), 1)
     for k, (r, c) in enumerate(CORNERS):
@@ -122,9 +158,9 @@
             mine = (lane8 >= 32 * q) & (lane8 < 32 * q + 32)
             rows = pl.ds((0 if r < 0 else 224) + 8 * q, 8)
             if c < 0:
-                part = pltpu.roll(codes_out[rows, 0:128], 32 * q, 1)
+                part = pltpu.roll(codes_v[rows, 0:128], 32 * q, 1)
             else:
-                part = pltpu.roll(codes_out[rows, 128:256], (32 * q + 32) % 128, 1)
+                part = pltpu.roll(codes_v[rows, 128:256], (32 * q + 32) % 128, 1)
             piece = jnp.where(mine, part, piece)
         corner_send[k, 0:8, :] = piece
         first = 16 if r < 0 else 256
@@ -136,26 +172,8 @@
             upper = pltpu.roll(upper, 64, 1)
         corner_send[k, 8:32, :] = jnp.where(lane24 < 64, upper, lower).astype(I32)
 
-    pl.semaphore_wait(barrier, 8)
-    copies = []
-
-    def send(source, target, step):
-        k = len(copies)
-        copy = pltpu.make_async_remote_copy(
-            source, target, send_sem.at[k], recv_sem.at[k],
-            device_id=device(step), device_id_type=MESH,
-        )
-        copy.start()
-        copies.append(copy)
-
-    send(w_send, e_out, (0, -1))
-    send(e_send, w_out, (0, 1))
     for k, step in enumerate(CORNERS):
         send(corner_send.at[k], corner_out.at[3 - k], step)
-    for k in (1, 2, 0, 3):
-        send(cells_v, lists_out.at[3 - k], SIDES[k])
-    send(codes_out.at[pl.ds(0, 32)], s_out, (-1, 0))
-    send(codes_out.at[pl.ds(224, 32)], n_out, (1, 0))
 
     loads[3].wait()
     block = (row * 1639) >> 16
@@ -165,7 +183,7 @@
     for k in range(16):
         part = slice(k * LANES, (k + 1) * LANES)
         index_out[k : k + 1, :] = place[:, part]
-        select_out[:, part] = one(iota((LANES, LANES), 0) == lane_of[:, part], BF16)
+        select_out[part, :] = jnp.broadcast_to(lane_of[:, part], (LANES, LANES)).T
 
     slot = iota((384, LANES), 0)
     code_col = jnp.where(slot < 256, slot + HALO, jnp.where(slot < 288, slot - 256, slot))
@@ -184,31 +202,60 @@
         column = jnp.where((column >= 0) & (column < TILE), column + (in_lane >> 5) * TILE, -1)
         for k in range(8):
             back_out[part, k * LANES : (k + 1) * LANES] = one(column == to_lane + k * LANES, BF16)
+
+    for copy in copies[4:8]:
+        copy.wait_recv()
+    for k, first, step in ((0, 0, -1), (1, FAR, 1)):
+        cells = lists_v[k]
+        row = (cells >> 9) + step * TILE
+        col = cells & (STRIDE - 1)
+        targets = [hot(inner_slots(col), 256), hot(slots(col, 0, FAR), 128)]
+        part = dot(hot(row - first, EDGE), jnp.concatenate(targets, axis=0), NT)
+        band = slice(first, first + EDGE)
+        for c in range(2):
+            count_v[c, band, :] += part[:, c * LANES : (c + 1) * LANES]
+        edge_out[band, :] += part[:, 256:384]
+    for c in range(2):
+        part = slice(c * LANES, (c + 1) * LANES)
+        wide_v[c, 0:32, :] = n_v[:, part].astype(F32)
+        wide_v[c, 32:288, :] = codes_v[:, part].astype(F32)
+        wide_v[c, 288:320, :] = s_v[:, part].astype(F32)
+    high, low = limbs(interleaved(count_v, 2))
+    minus_out[...] = dot(high, spread_counts[0:256, :]) + dot(low, spread_counts[0:256, :])
+    code_out[...] = dot(interleaved(wide_v, 2).astype(BF16), spread_codes[0:256, :])
+    for k, copy in enumerate(copies):
+        if not 4 <= k < 8:
+            copy.wait_recv()
     for copy in copies:
-        copy.wait()
+        copy.wait_send()
 
 
 def exchange(codes, start, actions, task):
     return pl.pallas_call(
         exchange_kernel,
         out_shape=(
-            pltpu.VMEM((4, 1, AGENTS), I32),
-            pltpu.VMEM((32, TILE), I32),
-            pltpu.VMEM((32, TILE), I32),
+            pltpu.VMEM((2, 1, AGENTS), I32),
             pltpu.VMEM((64, LANES), I32),
             pltpu.VMEM((64, LANES), I32),
             pltpu.VMEM((4, 32, LANES), I32),
-            pltpu.VMEM((TILE, TILE), I32),
-            pltpu.VMEM((3, EXT, LANES), F32),
+            pltpu.VMEM((EXT, LANES), F32),
+            pltpu.VMEM((EXT, WIDE), F32),
+            pltpu.VMEM((EXT, WIDE), F32),
             pltpu.VMEM((384, WIDE), BF16),
             pltpu.VMEM((384, WIDE), BF16),
             pltpu.VMEM((WIDE, 4 * TILE), BF16),
             pltpu.VMEM((16, LANES), I32),
-            pltpu.VMEM((LANES, AGENTS), BF16),
+            pltpu.VMEM((AGENTS, LANES), I32),
         ),
         in_specs=[pl.BlockSpec(memory_space=pltpu.HBM)] * 4,
-        out_specs=[pl.BlockSpec(memory_space=pltpu.VMEM)] * 13,
+        out_specs=[pl.BlockSpec(memory_space=pltpu.VMEM)] * 12,
         scratch_shapes=[
+            pltpu.VMEM((2, 1, AGENTS), I32),
+            pltpu.VMEM((32, TILE), I32),
+            pltpu.VMEM((32, TILE), I32),
+            pltpu.VMEM((TILE, TILE), I32),
+            pltpu.VMEM((2, EXT, LANES), F32),
+            pltpu.VMEM((2, EXT, LANES), F32),
             pltpu.VMEM((1, AGENTS), I32),
             pltpu.VMEM((16, AGENTS), I32),
             pltpu.VMEM((1, AGENTS), I32),
@@ -228,10 +275,10 @@
 
 
 def frame_kernel(
-    lists_ref, n_ref, s_ref, w_ref, e_ref, corner_ref, codes_ref, own_ref,
+    lists_ref, w_ref, e_ref, corner_ref, own_ref, code_ref, minus_ref,
     spread_codes, spread_counts, back_ref, index_v, select_ref, table_hbm,
     values_out, agent_out,
-    codes_v, count_v, reward_v, decay_v, val_a, val_b, natural_v, picked_v,
+    edge_v, reward_v, decay_v, val_a, val_b, natural_v, picked_v,
     index_s, table_ref, out_sem, index_sem, table_sem,
 ):
     to_smem = pltpu.make_async_copy(index_v, index_s, index_sem)
@@ -239,64 +286,39 @@
     to_table = pltpu.make_async_copy(table_hbm, table_ref, table_sem)
     to_table.start()
 
-    def cells_of(k):
+    edges = own_ref[...]
+    for k, step in ((0, -1), (1, 1)):
         cells = lists_ref[k]
-        step = SIDES[k]
-        return (cells >> 9) + step[0] * TILE, (cells & (STRIDE - 1)) + step[1] * TILE
-
-    row, col = cells_of(1)
-    edges = own_ref[2] + dot(hot(row, EXT), hot(slots(col, 0, FAR), 128), NT)
-    row, col = cells_of(2)
-    count_v[2] = edges + dot(hot(row, EXT), hot(slots(col, 0, FAR), 128), NT)
-    count_v[0] = own_ref[0]
-    count_v[1] = own_ref[1]
+        row = cells >> 9
+        col = (cells & (STRIDE - 1)) + step * TILE
+        edges += dot(hot(row, EXT), hot(slots(col, 0, FAR), 128), NT)
+    edge_v[0] = edges
     lane24 = iota((24, LANES), 1)
-    for k, first, pair in ((0, 0, 0), (3, FAR, 2)):
-        row, col = cells_of(k)
-        targets = [hot(inner_slots(col), 256), hot(slots(col, 0, FAR), 128)]
-        part = dot(hot(row - first, EDGE), jnp.concatenate(targets, axis=0), NT)
-        band = slice(first, first + EDGE)
-        for c in range(3):
-            count_v[c, band, :] += part[:, c * LANES : (c + 1) * LANES]
-        west = corner_ref[pair, 8:32, :].astype(F32)
-        east = corner_ref[pair + 1, 8:32, :].astype(F32)
+    for first, pair_at in ((0, 0), (FAR, 2)):
+        west = corner_ref[pair_at, 8:32, :].astype(F32)
+        east = corner_ref[pair_at + 1, 8:32, :].astype(F32)
         west2 = pltpu.roll(west, 64, 1)
         east2 = pltpu.roll(east, 64, 1)
-        count_v[2, first : first + 24, :] += jnp.where(lane24 < 64, west, east2)
-        count_v[2, first + 24 : first + 48, :] += jnp.where(lane24 < 64, west2, east)
-
-    for c in range(2):
-        part = pl.ds(c * LANES, LANES)
-        codes_v[c, 0:32, :] = n_ref[:, part].astype(F32)
-        codes_v[c, 32:288, :] = codes_ref[:, part].astype(F32)
-        codes_v[c, 288:320, :] = s_ref[:, part].astype(F32)
+        edge_v[0, first : first + 24, :] += jnp.where(lane24 < 64, west, east2)
+        edge_v[0, first + 24 : first + 48, :] += jnp.where(lane24 < 64, west2, east)
+
     lane = iota((64, LANES), 1)
     for q in range(4):
         west = pltpu.roll(w_ref[...], (128 - 32 * q) % 128, 1)
         east = pltpu.roll(e_ref[...], (160 - 32 * q) % 128, 1)
         both = jnp.where(lane < 32, west, jnp.where(lane < 64, east, 0))
-        codes_v[2, 32 + 64 * q : 96 + 64 * q, :] = both.astype(F32)
-        for first, pair in ((0, 0), (288, 2)):
-            west = pltpu.roll(corner_ref[pair, 0:8, :], (128 - 32 * q) % 128, 1)
-            east = pltpu.roll(corner_ref[pair + 1, 0:8, :], (160 - 32 * q) % 128, 1)
+        edge_v[1, 32 + 64 * q : 96 + 64 * q, :] = both.astype(F32)
+        for first, pair_at in ((0, 0), (288, 2)):
+            west = pltpu.roll(corner_ref[pair_at, 0:8, :], (128 - 32 * q) % 128, 1)
+            east = pltpu.roll(corner_ref[pair_at + 1, 0:8, :], (160 - 32 * q) % 128, 1)
             both = jnp.where(lane[0:8] < 32, west, jnp.where(lane[0:8] < 64, east, 0))
-            codes_v[2, first + 8 * q : first + 8 * q + 8, :] = both.astype(F32)
-
-    def interleaved(ref):
-        return jnp.concatenate(
-            [
-                jnp.concatenate([ref[c, pl.ds(i, 8, stride=ROWS), :] for i in range(ROWS)], axis=0)
-                for c in range(3)
-            ],
-            axis=1,
-        )
-
-    counts = interleaved(count_v)
-    high = jnp.floor(counts * (1.0 / 128.0))
-    low = counts - high * 128.0
-    minus = dot((high * (-128.0 * PENALTY)).astype(BF16), spread_counts[...])
-    minus += dot((low * -PENALTY).astype(BF16), spread_counts[...])
-    wide = dot(interleaved(codes_v).astype(BF16), spread_codes[...])
+            edge_v[1, first + 8 * q : first + 8 * q + 8, :] = both.astype(F32)
+
+    last = interleaved(edge_v, 2)
+    high, low = limbs(last[:, 0:LANES])
+    spread = spread_counts[256:384, :]
+    minus = dot(jnp.concatenate([high, low], axis=1), jnp.concatenate([spread, spread], axis=0))
+    wide = dot(last[:, LANES:].astype(BF16), spread_codes[256:384, :])
 
     to_table.wait()
     lane8 = iota((8, LANES), 1)
@@ -307,14 +329,15 @@
     shift = (lane8 // TASK_LANES % 2) * CODES
     for i in range(ROWS):
         for j in range(COLS):
-            code = wide[8 * i : 8 * i + 8, LANES * j : LANES * (j + 1)].astype(I32)
+            block = slice(8 * i, 8 * i + 8), slice(LANES * j, LANES * (j + 1))
+            code = (wide[block] + code_ref[block]).astype(I32)
             at = code + shift
             found = jnp.where(
                 lane8 < 64,
                 jnp.take_along_axis(table[0], at, axis=1),
                 jnp.take_along_axis(table[1], at, axis=1),
             )
-            reward = found + minus[8 * i : 8 * i + 8, LANES * j : LANES * (j + 1)]
+            reward = found + (minus[block] + minus_ref[block])
             spot = pl.ds((i * COLS + j) * 8, 8)
             reward_v[spot, :] = reward
             decay_v[spot, :] = jnp.where(code < CODES - TERMINAL, GAMMA, 0.0)
@@ -331,24 +354,24 @@
         put(ref, 0, [pltpu.roll(x, 1, 0) for x in take(ref, ROWS)])
         put(ref, ROWS + 1, [pltpu.roll(x, 7, 0) for x in take(ref, 1)])
 
-    def sides_of(now):
-        return pltpu.roll(now[COLS - 1], 1, 1), pltpu.roll(now[0], LANES - 1, 1)
+    def pair(above, now):
+        right = now[1:] + [pltpu.roll(now[0], LANES - 1, 1)]
+        return [jnp.maximum(a, b) for a, b in zip(above, right)]
 
     def sweep(source, target):
-        above, now = take(source, 0), take(source, 1)
-        outer = sides_of(now)
+        now = take(source, 1)
+        here = pair(take(source, 0), now)
         for i in range(ROWS):
             below = take(source, i + 2)
-            left = [outer[0]] + now[:-1]
-            right = now[1:] + [outer[1]]
+            under = pair(now, below)
+            other = [pltpu.roll(under[COLS - 1], 1, 1)] + under[:-1]
             new = []
             for j in range(COLS):
-                best = jnp.maximum(jnp.maximum(above[j], below[j]), jnp.maximum(left[j], right[j]))
                 spot = pl.ds((i * COLS + j) * 8, 8)
+                best = jnp.maximum(here[j], other[j])
                 new.append(reward_v[spot, :] + decay_v[spot, :] * best)
             put(target, i + 1, new)
-            above, now = now, below
-            outer = sides_of(now)
+            now, here = below, under
         wrap(target)
 
     wrap(val_a)
@@ -398,14 +421,19 @@
     lax.fori_loop(0, 16, pick, 0)
     diagonal = iota((LANES, LANES), 0) == iota((LANES, LANES), 1)
     for k in range(16):
-        rows = picked_v[k * LANES : (k + 1) * LANES, :]
-        upper = rows.astype(BF16)
-        lower = (rows - upper.astype(F32)).astype(BF16)
-        select = select_ref[:, k * LANES : (k + 1) * LANES]
-        crossed = dot(upper, select) + dot(lower, select)
-        agent_out[:, k * LANES : (k + 1) * LANES] = jnp.sum(
-            jnp.where(diagonal, crossed, 0.0), axis=0, keepdims=True
+        part = slice(k * LANES, (k + 1) * LANES)
+        found = jnp.concatenate(
+            [
+                jnp.take_along_axis(
+                    picked_v[k * LANES + 8 * a : k * LANES + 8 * a + 8, :],
+                    select_ref[k * LANES + 8 * a : k * LANES + 8 * a + 8, :],
+                    axis=1,
+                )
+                for a in range(16)
+            ],
+            axis=0,
         )
+        agent_out[:, part] = jnp.sum(jnp.where(diagonal, found, 0.0), axis=0, keepdims=True)
     for store in stores:
         store.wait()
 
@@ -417,11 +445,10 @@
             jax.ShapeDtypeStruct((4, TILE, TILE), F32),
             jax.ShapeDtypeStruct((1, AGENTS), F32),
         ),
-        in_specs=[pl.BlockSpec(memory_space=pltpu.VMEM)] * 13 + [pl.BlockSpec(memory_space=pltpu.HBM)],
+        in_specs=[pl.BlockSpec(memory_space=pltpu.VMEM)] * 12 + [pl.BlockSpec(memory_space=pltpu.HBM)],
         out_specs=[pl.BlockSpec(memory_space=pltpu.HBM), pl.BlockSpec(memory_space=pltpu.VMEM)],
         scratch_shapes=[
-            pltpu.VMEM((3, EXT, LANES), F32),
-            pltpu.VMEM((3, EXT, LANES), F32),
+            pltpu.VMEM((2, EXT, LANES), F32),
             pltpu.VMEM((ROWS * COLS * 8, LANES), F32),
             pltpu.VMEM((ROWS * COLS * 8, LANES), F32),
             pltpu.VMEM(((ROWS + 2) * COLS * 8, LANES), F32),

time: 31.8 us -> 30.1 us (0.947)
  Pallas kernels: 31 us -> 29.3 us
    pallas_call x1, Pallas kernels: 15.8 us -> 13.6 us  [frame(): pl.pallas_call(frame_kernel, out_shape=(jax.ShapeDtypeStruct((4, TILE, TI...]
    pallas_call x1, Pallas kernels: 15.2 us -> 15.8 us  [exchange(): pl.pallas_call(exchange_kernel, out_shape=(pltpu.VMEM((2, 1, AGENTS), I32...]
where the time goes in v4:
time: 30.1 us; the launch traced here: 30 us
  Pallas kernels  29.3 us (97%)
  between operations  0.64 us (2%)
    pallas_call x1, Pallas kernels, exchange(): pl.pallas_call(exchange_kernel, out_shape=(pltpu.VMEM((2, 1, AGENTS), I32...  15.8 us
    pallas_call x1, Pallas kernels, frame(): pl.pallas_call(frame_kernel, out_shape=(jax.ShapeDtypeStruct((4, TILE, TI...  13.6 us

profile of v4, /device:TPU:1, one launch (start us, length us, event | category | flops | bytes accessed | tf_op | source)
XLA Modules:
  0.0 30.0 jit_solution(14826387028463977843)
XLA Ops:
  0.6 15.8 %exchange.1 = (s32[2,1,2048]{2,1,0:T(1,128)S(1)}, s32[64,128]{1,0:T(8,128)S(1)}, s32[64,128]{1,0:T(8,128)S(1)}, s32[4,32,128]{2,1,0:T(8,128)S(1)}, f32[320,128]{...) custom-call(s32[1,2048]{1,0:T(1,128)} %bitcast.3, ...), custom_call_target="tpu_custom_call" | custom-call | tf_op jit(solution)/shard_map/exchange/pallas_call | solution.py:234
  16.4 13.6 %frame.1 = (f32[4,256,256]{2,1,0:T(8,128)}, f32[1,2048]{1,0:T(1,128)}) custom-call(s32[2,1,2048]{2,1,0:T(1,128)S(1)} %get-tuple-element.16.lists_ref, s32[64,128]{1,0:T(8,128)S(1)} %get-tuple-element.17.w_ref, s32[64,128]{1,0:T(8,128)S(1)} %get-tuple-element.18.e_ref, s32[4,32,128]{2,1,0:T(8,128)S(1)} %get-tuple-element.19.corner_ref, ...), custom_call_target="tpu_custom_call" | custom-call | tf_op jit(solution)/shard_map/frame/pallas_call | solution.py:442

commit v5 on v4

--- a/solution.py
+++ b/solution.py
@@ -20,10 +20,11 @@
 HALO = 32
 EXT = TILE + 2 * HALO
 ROWS = EXT // 8
-COLS = 10
+COLS = 5
 LANES = 128
-TASK_LANES = 32
+TASK_LANES = 64
 WIDE = COLS * LANES
+BOTH = 2 * COLS
 AGENTS = 2048
 STRIDE = 512
 EDGE = 48
@@ -177,9 +178,11 @@
 
     loads[3].wait()
     block = (row * 1639) >> 16
-    group = (col * 6554) >> 16
-    place = ((row - block * ROWS + 1) * COLS + (col - group * COLS)) * 8 + block
-    lane_of = task_v[...] * TASK_LANES + group
+    group = (col * 13108) >> 16
+    task = task_v[...]
+    place = (row - block * ROWS + 1) * BOTH + (task >> 1) * COLS + (col - group * COLS)
+    place = place * 8 + block
+    lane_of = (task & 1) * TASK_LANES + group
     for k in range(16):
         part = slice(k * LANES, (k + 1) * LANES)
         index_out[k : k + 1, :] = place[:, part]
@@ -191,16 +194,16 @@
     count_col = jnp.where(slot < FAR - EDGE, slot + EDGE, -1)
     count_col = jnp.where((slot >= 256) & (slot < 256 + EDGE), slot - 256, count_col)
     count_col = jnp.where((slot >= 320) & (slot < 320 + EDGE), slot - 320 + FAR, count_col)
-    first_col = (iota((1, LANES), 1) & 31) * COLS
+    first_col = (iota((1, LANES), 1) & 63) * COLS
     in_lane = iota((LANES, LANES), 0)
     to_lane = iota((LANES, LANES), 1)
     for j in range(COLS):
         part = slice(j * LANES, (j + 1) * LANES)
         spread_codes[:, part] = one(code_col == first_col + j, BF16)
         spread_counts[:, part] = one(count_col == first_col + j, BF16)
-        column = (in_lane & 31) * COLS + (j - HALO)
-        column = jnp.where((column >= 0) & (column < TILE), column + (in_lane >> 5) * TILE, -1)
-        for k in range(8):
+        column = (in_lane & 63) * COLS + (j - HALO)
+        column = jnp.where((column >= 0) & (column < TILE), column + (in_lane >> 6) * TILE, -1)
+        for k in range(4):
             back_out[part, k * LANES : (k + 1) * LANES] = one(column == to_lane + k * LANES, BF16)
 
     for copy in copies[4:8]:
@@ -243,7 +246,7 @@
             pltpu.VMEM((EXT, WIDE), F32),
             pltpu.VMEM((384, WIDE), BF16),
             pltpu.VMEM((384, WIDE), BF16),
-            pltpu.VMEM((WIDE, 4 * TILE), BF16),
+            pltpu.VMEM((WIDE, 2 * TILE), BF16),
             pltpu.VMEM((16, LANES), I32),
             pltpu.VMEM((AGENTS, LANES), I32),
         ),
@@ -326,52 +329,56 @@
     for k in range(2):
         pair = jnp.concatenate([table_ref[2 * k : 2 * k + 1, :], table_ref[2 * k + 1 : 2 * k + 2, :]], axis=1)
         table.append(jnp.broadcast_to(pair, (8, LANES)))
-    shift = (lane8 // TASK_LANES % 2) * CODES
+    shift = (lane8 >> 6) * CODES
     for i in range(ROWS):
         for j in range(COLS):
             block = slice(8 * i, 8 * i + 8), slice(LANES * j, LANES * (j + 1))
             code = (wide[block] + code_ref[block]).astype(I32)
             at = code + shift
-            found = jnp.where(
-                lane8 < 64,
-                jnp.take_along_axis(table[0], at, axis=1),
-                jnp.take_along_axis(table[1], at, axis=1),
-            )
-            reward = found + (minus[block] + minus_ref[block])
-            spot = pl.ds((i * COLS + j) * 8, 8)
-            reward_v[spot, :] = reward
-            decay_v[spot, :] = jnp.where(code < CODES - TERMINAL, GAMMA, 0.0)
-            val_a[pl.ds(((i + 1) * COLS + j) * 8, 8), :] = reward
+            less = minus[block] + minus_ref[block]
+            decay_v[pl.ds((i * COLS + j) * 8, 8), :] = jnp.where(code < CODES - TERMINAL, GAMMA, 0.0)
+            for p in range(2):
+                reward = jnp.take_along_axis(table[p], at, axis=1) + less
+                reward_v[pl.ds((i * BOTH + p * COLS + j) * 8, 8), :] = reward
+                val_a[pl.ds(((i + 1) * BOTH + p * COLS + j) * 8, 8), :] = reward
 
     def take(ref, i):
-        return [ref[pl.ds((i * COLS + j) * 8, 8), :] for j in range(COLS)]
+        return [ref[pl.ds((i * BOTH + j) * 8, 8), :] for j in range(BOTH)]
 
     def put(ref, i, vregs):
-        for j in range(COLS):
-            ref[pl.ds((i * COLS + j) * 8, 8), :] = vregs[j]
+        for j in range(BOTH):
+            ref[pl.ds((i * BOTH + j) * 8, 8), :] = vregs[j]
 
     def wrap(ref):
         put(ref, 0, [pltpu.roll(x, 1, 0) for x in take(ref, ROWS)])
         put(ref, ROWS + 1, [pltpu.roll(x, 7, 0) for x in take(ref, 1)])
 
-    def pair(above, now):
-        right = now[1:] + [pltpu.roll(now[0], LANES - 1, 1)]
+    def ends(row):
+        first = [pltpu.roll(row[p], LANES - 1, 1) for p in (0, COLS)]
+        last = [pltpu.roll(row[p + COLS - 1], 1, 1) for p in (0, COLS)]
+        return first, last
+
+    def pair(above, now, first):
+        right = now[1:COLS] + [first[0]] + now[COLS + 1 :] + [first[1]]
         return [jnp.maximum(a, b) for a, b in zip(above, right)]
 
     def sweep(source, target):
         now = take(source, 1)
-        here = pair(take(source, 0), now)
+        first, last = ends(now)
+        here = pair(take(source, 0), now, first)
         for i in range(ROWS):
             below = take(source, i + 2)
-            under = pair(now, below)
-            other = [pltpu.roll(under[COLS - 1], 1, 1)] + under[:-1]
-            new = []
+            first, next_last = ends(below)
+            under = pair(now, below, first)
+            new = [None] * BOTH
             for j in range(COLS):
-                spot = pl.ds((i * COLS + j) * 8, 8)
-                best = jnp.maximum(here[j], other[j])
-                new.append(reward_v[spot, :] + decay_v[spot, :] * best)
+                decay = decay_v[pl.ds((i * COLS + j) * 8, 8), :]
+                for k, p in enumerate((0, COLS)):
+                    other = under[p + j - 1] if j else jnp.maximum(last[k], below[p])
+                    reward = reward_v[pl.ds((i * BOTH + p + j) * 8, 8), :]
+                    new[p + j] = reward + decay * jnp.maximum(here[p + j], other)
             put(target, i + 1, new)
-            now, here = below, under
+            now, here, last = below, under, next_last
         wrap(target)
 
     wrap(val_a)
@@ -383,33 +390,29 @@
 
     lax.fori_loop(0, SWEEPS // 2, two_sweeps, 0)
 
-    block = jnp.concatenate(
-        [
-            jnp.concatenate(
-                [val_a[pl.ds(((i + 1) * COLS + j) * 8, 8), :] for i in range(ROWS)], axis=0
+    back = back_ref[...]
+    stores = []
+    for p in range(2):
+        parts = []
+        for j in range(COLS):
+            rows = [val_a[pl.ds(((i + 1) * BOTH + p * COLS + j) * 8, 8), :] for i in range(ROWS)]
+            parts.append(jnp.concatenate(rows, axis=0))
+        block = jnp.concatenate(parts, axis=1)
+        upper = block.astype(BF16)
+        lower = (block - upper.astype(F32)).astype(BF16)
+        flat = dot(upper, back) + dot(lower, back)
+        for c in range(4):
+            for i in range(ROWS):
+                piece = flat[8 * i : 8 * i + 8, c * LANES : (c + 1) * LANES]
+                natural_v[4 * p + c, pl.ds(i, 8, stride=ROWS), :] = piece
+            stores.append(
+                pltpu.make_async_copy(
+                    natural_v.at[4 * p + c, pl.ds(HALO, TILE)],
+                    values_out.at[2 * p + c // 2, :, pl.ds(c % 2 * LANES, LANES)],
+                    out_sem.at[4 * p + c],
+                )
             )
-            for j in range(COLS)
-        ],
-        axis=1,
-    )
-    upper = block.astype(BF16)
-    lower = (block - upper.astype(F32)).astype(BF16)
-    back = back_ref[...]
-    flat = dot(upper, back) + dot(lower, back)
-    for i in range(ROWS):
-        for c in range(8):
-            piece = flat[8 * i : 8 * i + 8, c * LANES : (c + 1) * LANES]
-            natural_v[c, pl.ds(i, 8, stride=ROWS), :] = piece
-    stores = []
-    for c in range(8):
-        stores.append(
-            pltpu.make_async_copy(
-                natural_v.at[c, pl.ds(HALO, TILE)],
-                values_out.at[c // 2, :, pl.ds(c % 2 * LANES, LANES)],
-                out_sem.at[c],
-            )
-        )
-        stores[-1].start()
+            stores[-1].start()
 
     to_smem.wait()
 
@@ -449,10 +452,10 @@
         out_specs=[pl.BlockSpec(memory_space=pltpu.HBM), pl.BlockSpec(memory_space=pltpu.VMEM)],
         scratch_shapes=[
             pltpu.VMEM((2, EXT, LANES), F32),
+            pltpu.VMEM((ROWS * BOTH * 8, LANES), F32),
             pltpu.VMEM((ROWS * COLS * 8, LANES), F32),
-            pltpu.VMEM((ROWS * COLS * 8, LANES), F32),
-            pltpu.VMEM(((ROWS + 2) * COLS * 8, LANES), F32),
-            pltpu.VMEM(((ROWS + 2) * COLS * 8, LANES), F32),
+            pltpu.VMEM(((ROWS + 2) * BOTH * 8, LANES), F32),
+            pltpu.VMEM(((ROWS + 2) * BOTH * 8, LANES), F32),
             pltpu.VMEM((8, EXT, LANES), F32),
             pltpu.VMEM((AGENTS, LANES), F32),
             pltpu.SMEM((16, LANES), I32),

time: 30.1 us -> 29.1 us (0.967)
  Pallas kernels: 29.3 us -> 28.3 us
    pallas_call x1, Pallas kernels: 13.6 us -> 12.5 us  [frame(): pl.pallas_call(frame_kernel, out_shape=(jax.ShapeDtypeStruct((4, TILE, TI...]
where the time goes in v5:
time: 29.1 us; the launch traced here: 28.9 us
  Pallas kernels  28.3 us (97%)
  between operations  0.64 us (2%)
    pallas_call x1, Pallas kernels, exchange(): pl.pallas_call(exchange_kernel, out_shape=(pltpu.VMEM((2, 1, AGENTS), I32...  15.8 us
    pallas_call x1, Pallas kernels, frame(): pl.pallas_call(frame_kernel, out_shape=(jax.ShapeDtypeStruct((4, TILE, TI...  12.5 us

profile of v5, /device:TPU:1, one launch (start us, length us, event | category | flops | bytes accessed | tf_op | source)
XLA Modules:
  0.0 28.9 jit_solution(596251993922745811)
XLA Ops:
  0.6 15.8 %exchange.1 = (s32[2,1,2048]{2,1,0:T(1,128)S(1)}, s32[64,128]{1,0:T(8,128)S(1)}, s32[64,128]{1,0:T(8,128)S(1)}, s32[4,32,128]{2,1,0:T(8,128)S(1)}, f32[320,128]{...) custom-call(s32[1,2048]{1,0:T(1,128)} %bitcast.3, ...), custom_call_target="tpu_custom_call" | custom-call | tf_op jit(solution)/shard_map/exchange/pallas_call | solution.py:237
  16.4 12.5 %frame.1 = (f32[4,256,256]{2,1,0:T(8,128)}, f32[1,2048]{1,0:T(1,128)}) custom-call(s32[2,1,2048]{2,1,0:T(1,128)S(1)} %get-tuple-element.16.lists_ref, s32[64,128]{1,0:T(8,128)S(1)} %get-tuple-element.17.w_ref, s32[64,128]{1,0:T(8,128)S(1)} %get-tuple-element.18.e_ref, s32[4,32,128]{2,1,0:T(8,128)S(1)} %get-tuple-element.19.corner_ref, ...), custom_call_target="tpu_custom_call" | custom-call | tf_op jit(solution)/shard_map/frame/pallas_call | solution.py:445

commit v6 on v5

--- a/solution.py
+++ b/solution.py
@@ -81,7 +81,7 @@
 
 def exchange_kernel(
     start_hbm, act_hbm, codes_hbm, task_hbm,
-    side_out, w_out, e_out, corner_out, edge_out, code_out, minus_out,
+    w_out, e_out, corner_out, edge_out, code_out, minus_out,
     spread_codes, spread_counts, back_out, index_out, select_out,
     lists_v, n_v, s_v, codes_v, count_v, wide_v, start_v, act_v, task_v, cells_v, w_send, e_send, corner_send, local_sem, send_sem, recv_sem,
 ):
@@ -136,8 +136,8 @@
         copy.start()
         copies.append(copy)
 
-    send(cells_v, side_out.at[1], (0, -1))
-    send(cells_v, side_out.at[0], (0, 1))
+    send(cells_v, lists_v.at[3], (0, -1))
+    send(cells_v, lists_v.at[2], (0, 1))
     send(w_send, e_out, (0, -1))
     send(e_send, w_out, (0, 1))
     send(cells_v, lists_v.at[1], (-1, 0))
@@ -226,8 +226,13 @@
     high, low = limbs(interleaved(count_v, 2))
     minus_out[...] = dot(high, spread_counts[0:256, :]) + dot(low, spread_counts[0:256, :])
     code_out[...] = dot(interleaved(wide_v, 2).astype(BF16), spread_codes[0:256, :])
+    for k, step in ((0, 1), (1, -1)):
+        copies[k].wait_recv()
+        cells = lists_v[3 - k]
+        col = (cells & (STRIDE - 1)) + step * TILE
+        edge_out[...] += dot(hot(cells >> 9, EXT), hot(slots(col, 0, FAR), 128), NT)
     for k, copy in enumerate(copies):
-        if not 4 <= k < 8:
+        if k in (2, 3) or k >= 8:
             copy.wait_recv()
     for copy in copies:
         copy.wait_send()
@@ -237,7 +242,6 @@
     return pl.pallas_call(
         exchange_kernel,
         out_shape=(
-            pltpu.VMEM((2, 1, AGENTS), I32),
             pltpu.VMEM((64, LANES), I32),
             pltpu.VMEM((64, LANES), I32),
             pltpu.VMEM((4, 32, LANES), I32),
@@ -251,9 +255,9 @@
             pltpu.VMEM((AGENTS, LANES), I32),
         ),
         in_specs=[pl.BlockSpec(memory_space=pltpu.HBM)] * 4,
-        out_specs=[pl.BlockSpec(memory_space=pltpu.VMEM)] * 12,
+        out_specs=[pl.BlockSpec(memory_space=pltpu.VMEM)] * 11,
         scratch_shapes=[
-            pltpu.VMEM((2, 1, AGENTS), I32),
+            pltpu.VMEM((4, 1, AGENTS), I32),
             pltpu.VMEM((32, TILE), I32),
             pltpu.VMEM((32, TILE), I32),
             pltpu.VMEM((TILE, TILE), I32),
@@ -278,7 +282,7 @@
 
 
 def frame_kernel(
-    lists_ref, w_ref, e_ref, corner_ref, own_ref, code_ref, minus_ref,
+    w_ref, e_ref, corner_ref, own_ref, code_ref, minus_ref,
     spread_codes, spread_counts, back_ref, index_v, select_ref, table_hbm,
     values_out, agent_out,
     edge_v, reward_v, decay_v, val_a, val_b, natural_v, picked_v,
@@ -289,13 +293,7 @@
     to_table = pltpu.make_async_copy(table_hbm, table_ref, table_sem)
     to_table.start()
 
-    edges = own_ref[...]
-    for k, step in ((0, -1), (1, 1)):
-        cells = lists_ref[k]
-        row = cells >> 9
-        col = (cells & (STRIDE - 1)) + step * TILE
-        edges += dot(hot(row, EXT), hot(slots(col, 0, FAR), 128), NT)
-    edge_v[0] = edges
+    edge_v[0] = own_ref[...]
     lane24 = iota((24, LANES), 1)
     for first, pair_at in ((0, 0), (FAR, 2)):
         west = corner_ref[pair_at, 8:32, :].astype(F32)
@@ -389,6 +387,11 @@
         return carry
 
     lax.fori_loop(0, SWEEPS // 2, two_sweeps, 0)
+
+    to_smem.wait()
+    for k in range(16):
+        for a in range(LANES):
+            picked_v[pl.ds(k * LANES + a, 1), :] = val_a[pl.ds(index_s[k, a], 1), :]
 
     back = back_ref[...]
     stores = []
@@ -414,14 +417,6 @@
             )
             stores[-1].start()
 
-    to_smem.wait()
-
-    def pick(k, carry):
-        for a in range(LANES):
-            picked_v[pl.ds(k * LANES + a, 1), :] = val_a[pl.ds(index_s[k, a], 1), :]
-        return carry
-
-    lax.fori_loop(0, 16, pick, 0)
     diagonal = iota((LANES, LANES), 0) == iota((LANES, LANES), 1)
     for k in range(16):
         part = slice(k * LANES, (k + 1) * LANES)
@@ -448,7 +443,7 @@
             jax.ShapeDtypeStruct((4, TILE, TILE), F32),
             jax.ShapeDtypeStruct((1, AGENTS), F32),
         ),
-        in_specs=[pl.BlockSpec(memory_space=pltpu.VMEM)] * 12 + [pl.BlockSpec(memory_space=pltpu.HBM)],
+        in_specs=[pl.BlockSpec(memory_space=pltpu.VMEM)] * 11 + [pl.BlockSpec(memory_space=pltpu.HBM)],
         out_specs=[pl.BlockSpec(memory_space=pltpu.HBM), pl.BlockSpec(memory_space=pltpu.VMEM)],
         scratch_shapes=[
             pltpu.VMEM((2, EXT, LANES), F32),

time: 29.1 us -> 28.3 us (0.973)
  Pallas kernels: 28.3 us -> 27.6 us
    pallas_call x1, Pallas kernels: 12.5 us -> 10.8 us  [frame(): pl.pallas_call(frame_kernel, out_shape=(jax.ShapeDtypeStruct((4, TILE, TI...]
    pallas_call x1, Pallas kernels: 15.8 us -> 16.7 us  [exchange(): pl.pallas_call(exchange_kernel, out_shape=(pltpu.VMEM((64, LANES), I32),...]
where the time goes in v6:
time: 28.3 us; the launch traced here: 28.2 us
  Pallas kernels  27.6 us (98%)
  between operations  0.64 us (2%)
    pallas_call x1, Pallas kernels, exchange(): pl.pallas_call(exchange_kernel, out_shape=(pltpu.VMEM((64, LANES), I32),...  16.7 us
    pallas_call x1, Pallas kernels, frame(): pl.pallas_call(frame_kernel, out_shape=(jax.ShapeDtypeStruct((4, TILE, TI...  10.8 us

profile of v6, /device:TPU:1, one launch (start us, length us, event | category | flops | bytes accessed | tf_op | source)
XLA Modules:
  0.0 28.2 jit_solution(16134490613510415842)
XLA Ops:
  0.6 16.7 %exchange.1 = (s32[64,128]{1,0:T(8,128)S(1)}, s32[64,128]{1,0:T(8,128)S(1)}, s32[4,32,128]{2,1,0:T(8,128)S(1)}, f32[320,128]{1,0:T(8,128)S(1)}, f32[320,640]{1,0...) custom-call(s32[1,2048]{1,0:T(1,128)} %bitcast.3, ...), custom_call_target="tpu_custom_call" | custom-call | tf_op jit(solution)/shard_map/exchange/pallas_call | solution.py:242
  17.4 10.8 %frame.1 = (f32[4,256,256]{2,1,0:T(8,128)}, f32[1,2048]{1,0:T(1,128)}) custom-call(s32[64,128]{1,0:T(8,128)S(1)} %get-tuple-element.15.w_ref, s32[64,128]{1,0:T(8,128)S(1)} %get-tuple-element.16.e_ref, s32[4,32,128]{2,1,0:T(8,128)S(1)} %get-tuple-element.17.corner_ref, f32[320,128]{1,0:T(8,128)S(1)} %get-tuple-element.18.own_ref, ...), custom_call_target="tpu_custom_call" | custom-call | tf_op jit(solution)/shard_map/frame/pallas_call | solution.py:440

commit v7 on v6

--- a/solution.py
+++ b/solution.py
@@ -103,6 +103,24 @@
     for step in NEIGHBOURS:
         pl.semaphore_signal(barrier, inc=1, device_id=device(step), device_id_type=MESH)
 
+    slot = iota((384, LANES), 0)
+    code_col = jnp.where(slot < 256, slot + HALO, jnp.where(slot < 288, slot - 256, slot))
+    code_col = jnp.where(slot < 320, code_col, -1)
+    count_col = jnp.where(slot < FAR - EDGE, slot + EDGE, -1)
+    count_col = jnp.where((slot >= 256) & (slot < 256 + EDGE), slot - 256, count_col)
+    count_col = jnp.where((slot >= 320) & (slot < 320 + EDGE), slot - 320 + FAR, count_col)
+    first_col = (iota((1, LANES), 1) & 63) * COLS
+    in_lane = iota((LANES, LANES), 0)
+    to_lane = iota((LANES, LANES), 1)
+    for j in range(COLS):
+        part = slice(j * LANES, (j + 1) * LANES)
+        spread_codes[:, part] = one(code_col == first_col + j, BF16)
+        spread_counts[:, part] = one(count_col == first_col + j, BF16)
+        column = (in_lane & 63) * COLS + (j - HALO)
+        column = jnp.where((column >= 0) & (column < TILE), column + (in_lane >> 6) * TILE, -1)
+        for k in range(4):
+            back_out[part, k * LANES : (k + 1) * LANES] = one(column == to_lane + k * LANES, BF16)
+
     loads[0].wait()
     loads[1].wait()
     act = act_v[...]
@@ -112,6 +130,12 @@
     row += jnp.sum((act == 2).astype(I32) - (act == 1).astype(I32), axis=0, keepdims=True)
     col += jnp.sum((act == 4).astype(I32) - (act == 3).astype(I32), axis=0, keepdims=True)
     cells_v[...] = row * STRIDE + col
+
+    targets = [hot(inner_slots(col), 256), hot(slots(col, 0, FAR), 128), hot(slots(col, 16, 256), 128)]
+    own = dot(hot(row, EXT), jnp.concatenate(targets, axis=0), NT)
+    for c in range(2):
+        count_v[c] = own[:, c * LANES : (c + 1) * LANES]
+    edge_out[...] = own[:, 256:384]
 
     loads[2].wait()
     lane = iota((64, LANES), 1)
@@ -124,33 +148,6 @@
         east = jnp.where(mine, pltpu.roll(codes_v[rows, 128:256], (32 * q + 32) % 128, 1), east)
     w_send[...] = west
     e_send[...] = east
-    pl.semaphore_wait(barrier, 8)
-    copies = []
-
-    def send(source, target, step):
-        k = len(copies)
-        copy = pltpu.make_async_remote_copy(
-            source, target, send_sem.at[k], recv_sem.at[k],
-            device_id=device(step), device_id_type=MESH,
-        )
-        copy.start()
-        copies.append(copy)
-
-    send(cells_v, lists_v.at[3], (0, -1))
-    send(cells_v, lists_v.at[2], (0, 1))
-    send(w_send, e_out, (0, -1))
-    send(e_send, w_out, (0, 1))
-    send(cells_v, lists_v.at[1], (-1, 0))
-    send(cells_v, lists_v.at[0], (1, 0))
-    send(codes_v.at[pl.ds(0, 32)], s_v, (-1, 0))
-    send(codes_v.at[pl.ds(224, 32)], n_v, (1, 0))
-
-    targets = [hot(inner_slots(col), 256), hot(slots(col, 0, FAR), 128), hot(slots(col, 16, 256), 128)]
-    own = dot(hot(row, EXT), jnp.concatenate(targets, axis=0), NT)
-    for c in range(2):
-        count_v[c] = own[:, c * LANES : (c + 1) * LANES]
-    edge_out[...] = own[:, 256:384]
-
     lane8 = iota((8, LANES), 1)
     lane24 = iota((24, LANES), 1)
     for k, (r, c) in enumerate(CORNERS):
@@ -173,8 +170,28 @@
             upper = pltpu.roll(upper, 64, 1)
         corner_send[k, 8:32, :] = jnp.where(lane24 < 64, upper, lower).astype(I32)
 
+    pl.semaphore_wait(barrier, 8)
+    copies = []
+
+    def send(source, target, step):
+        k = len(copies)
+        copy = pltpu.make_async_remote_copy(
+            source, target, send_sem.at[k], recv_sem.at[k],
+            device_id=device(step), device_id_type=MESH,
+        )
+        copy.start()
+        copies.append(copy)
+
+    send(cells_v, lists_v.at[1], (-1, 0))
+    send(cells_v, lists_v.at[0], (1, 0))
+    send(codes_v.at[pl.ds(0, 32)], s_v, (-1, 0))
+    send(codes_v.at[pl.ds(224, 32)], n_v, (1, 0))
+    send(cells_v, lists_v.at[3], (0, -1))
+    send(cells_v, lists_v.at[2], (0, 1))
     for k, step in enumerate(CORNERS):
         send(corner_send.at[k], corner_out.at[3 - k], step)
+    send(w_send, e_out, (0, -1))
+    send(e_send, w_out, (0, 1))
 
     loads[3].wait()
     block = (row * 1639) >> 16
@@ -188,25 +205,7 @@
         index_out[k : k + 1, :] = place[:, part]
         select_out[part, :] = jnp.broadcast_to(lane_of[:, part], (LANES, LANES)).T
 
-    slot = iota((384, LANES), 0)
-    code_col = jnp.where(slot < 256, slot + HALO, jnp.where(slot < 288, slot - 256, slot))
-    code_col = jnp.where(slot < 320, code_col, -1)
-    count_col = jnp.where(slot < FAR - EDGE, slot + EDGE, -1)
-    count_col = jnp.where((slot >= 256) & (slot < 256 + EDGE), slot - 256, count_col)
-    count_col = jnp.where((slot >= 320) & (slot < 320 + EDGE), slot - 320 + FAR, count_col)
-    first_col = (iota((1, LANES), 1) & 63) * COLS
-    in_lane = iota((LANES, LANES), 0)
-    to_lane = iota((LANES, LANES), 1)
-    for j in range(COLS):
-        part = slice(j * LANES, (j + 1) * LANES)
-        spread_codes[:, part] = one(code_col == first_col + j, BF16)
-        spread_counts[:, part] = one(count_col == first_col + j, BF16)
-        column = (in_lane & 63) * COLS + (j - HALO)
-        column = jnp.where((column >= 0) & (column < TILE), column + (in_lane >> 6) * TILE, -1)
-        for k in range(4):
-            back_out[part, k * LANES : (k + 1) * LANES] = one(column == to_lane + k * LANES, BF16)
-
-    for copy in copies[4:8]:
+    for copy in copies[0:2] + copies[2:4]:
         copy.wait_recv()
     for k, first, step in ((0, 0, -1), (1, FAR, 1)):
         cells = lists_v[k]
@@ -227,13 +226,12 @@
     minus_out[...] = dot(high, spread_counts[0:256, :]) + dot(low, spread_counts[0:256, :])
     code_out[...] = dot(interleaved(wide_v, 2).astype(BF16), spread_codes[0:256, :])
     for k, step in ((0, 1), (1, -1)):
-        copies[k].wait_recv()
+        copies[4 + k].wait_recv()
         cells = lists_v[3 - k]
         col = (cells & (STRIDE - 1)) + step * TILE
         edge_out[...] += dot(hot(cells >> 9, EXT), hot(slots(col, 0, FAR), 128), NT)
-    for k, copy in enumerate(copies):
-        if k in (2, 3) or k >= 8:
-            copy.wait_recv()
+    for copy in copies[6:10] + copies[10:12]:
+        copy.wait_recv()
     for copy in copies:
         copy.wait_send()
 

time: 28.3 us -> 27.5 us (0.972)
  Pallas kernels: 27.6 us -> 26.7 us
    pallas_call x1, Pallas kernels: 16.7 us -> 15.9 us  [exchange(): pl.pallas_call(exchange_kernel, out_shape=(pltpu.VMEM((64, LANES), I32),...]
where the time goes in v7:
time: 27.5 us; the launch traced here: 27.4 us
  Pallas kernels  26.7 us (97%)
  between operations  0.64 us (2%)
    pallas_call x1, Pallas kernels, exchange(): pl.pallas_call(exchange_kernel, out_shape=(pltpu.VMEM((64, LANES), I32),...  15.9 us
    pallas_call x1, Pallas kernels, frame(): pl.pallas_call(frame_kernel, out_shape=(jax.ShapeDtypeStruct((4, TILE, TI...  10.8 us

profile of v7, /device:TPU:1, one launch (start us, length us, event | category | flops | bytes accessed | tf_op | source)
XLA Modules:
  0.0 27.4 jit_solution(11240128609519599640)
XLA Ops:
  0.6 15.9 %exchange.1 = (s32[64,128]{1,0:T(8,128)S(1)}, s32[64,128]{1,0:T(8,128)S(1)}, s32[4,32,128]{2,1,0:T(8,128)S(1)}, f32[320,128]{1,0:T(8,128)S(1)}, f32[320,640]{1,0...) custom-call(s32[1,2048]{1,0:T(1,128)} %bitcast.3, ...), custom_call_target="tpu_custom_call" | custom-call | tf_op jit(solution)/shard_map/exchange/pallas_call | solution.py:240
  16.5 10.8 %frame.1 = (f32[4,256,256]{2,1,0:T(8,128)}, f32[1,2048]{1,0:T(1,128)}) custom-call(s32[64,128]{1,0:T(8,128)S(1)} %get-tuple-element.15.w_ref, s32[64,128]{1,0:T(8,128)S(1)} %get-tuple-element.16.e_ref, s32[4,32,128]{2,1,0:T(8,128)S(1)} %get-tuple-element.17.corner_ref, f32[320,128]{1,0:T(8,128)S(1)} %get-tuple-element.18.own_ref, ...), custom_call_target="tpu_custom_call" | custom-call | tf_op jit(solution)/shard_map/frame/pallas_call | solution.py:438

commit v8 on v7

--- a/solution.py
+++ b/solution.py
@@ -384,7 +384,8 @@
         sweep(val_b, val_a)
         return carry
 
-    lax.fori_loop(0, SWEEPS // 2, two_sweeps, 0)
+    lax.fori_loop(0, SWEEPS // 2 - 1, two_sweeps, 0)
+    two_sweeps(0, 0)
 
     to_smem.wait()
     for k in range(16):

time: 27.5 us -> 26.7 us (0.971)
  Pallas kernels: 26.7 us -> 25.9 us
    pallas_call x1, Pallas kernels: 10.8 us -> 10 us  [frame(): pl.pallas_call(frame_kernel, out_shape=(jax.ShapeDtypeStruct((4, TILE, TI...]
where the time goes in v8:
time: 26.7 us; the launch traced here: 26.6 us
  Pallas kernels  25.9 us (97%)
  between operations  0.64 us (2%)
    pallas_call x1, Pallas kernels, exchange(): pl.pallas_call(exchange_kernel, out_shape=(pltpu.VMEM((64, LANES), I32),...  15.9 us
    pallas_call x1, Pallas kernels, frame(): pl.pallas_call(frame_kernel, out_shape=(jax.ShapeDtypeStruct((4, TILE, TI...  10 us

profile of v8, /device:TPU:1, one launch (start us, length us, event | category | flops | bytes accessed | tf_op | source)
XLA Modules:
  0.0 26.6 jit_solution(16124562439991524391)
XLA Ops:
  0.6 15.9 %exchange.1 = (s32[64,128]{1,0:T(8,128)S(1)}, s32[64,128]{1,0:T(8,128)S(1)}, s32[4,32,128]{2,1,0:T(8,128)S(1)}, f32[320,128]{1,0:T(8,128)S(1)}, f32[320,640]{1,0...) custom-call(s32[1,2048]{1,0:T(1,128)} %bitcast.3, ...), custom_call_target="tpu_custom_call" | custom-call | tf_op jit(solution)/shard_map/exchange/pallas_call | solution.py:240
  16.5 10.0 %frame.1 = (f32[4,256,256]{2,1,0:T(8,128)}, f32[1,2048]{1,0:T(1,128)}) custom-call(s32[64,128]{1,0:T(8,128)S(1)} %get-tuple-element.15.w_ref, s32[64,128]{1,0:T(8,128)S(1)} %get-tuple-element.16.e_ref, s32[4,32,128]{2,1,0:T(8,128)S(1)} %get-tuple-element.17.corner_ref, f32[320,128]{1,0:T(8,128)S(1)} %get-tuple-element.18.own_ref, ...), custom_call_target="tpu_custom_call" | custom-call | tf_op jit(solution)/shard_map/frame/pallas_call | solution.py:439

commit v9 on v8

--- a/solution.py
+++ b/solution.py
@@ -131,12 +131,6 @@
     col += jnp.sum((act == 4).astype(I32) - (act == 3).astype(I32), axis=0, keepdims=True)
     cells_v[...] = row * STRIDE + col
 
-    targets = [hot(inner_slots(col), 256), hot(slots(col, 0, FAR), 128), hot(slots(col, 16, 256), 128)]
-    own = dot(hot(row, EXT), jnp.concatenate(targets, axis=0), NT)
-    for c in range(2):
-        count_v[c] = own[:, c * LANES : (c + 1) * LANES]
-    edge_out[...] = own[:, 256:384]
-
     loads[2].wait()
     lane = iota((64, LANES), 1)
     west = jnp.zeros((64, LANES), I32)
@@ -148,6 +142,33 @@
         east = jnp.where(mine, pltpu.roll(codes_v[rows, 128:256], (32 * q + 32) % 128, 1), east)
     w_send[...] = west
     e_send[...] = east
+    pl.semaphore_wait(barrier, 8)
+    copies = []
+
+    def send(source, target, step):
+        k = len(copies)
+        copy = pltpu.make_async_remote_copy(
+            source, target, send_sem.at[k], recv_sem.at[k],
+            device_id=device(step), device_id_type=MESH,
+        )
+        copy.start()
+        copies.append(copy)
+
+    send(cells_v, lists_v.at[1], (-1, 0))
+    send(cells_v, lists_v.at[0], (1, 0))
+    send(codes_v.at[pl.ds(0, 32)], s_v, (-1, 0))
+    send(codes_v.at[pl.ds(224, 32)], n_v, (1, 0))
+    send(cells_v, lists_v.at[3], (0, -1))
+    send(cells_v, lists_v.at[2], (0, 1))
+    send(w_send, e_out, (0, -1))
+    send(e_send, w_out, (0, 1))
+
+    targets = [hot(inner_slots(col), 256), hot(slots(col, 0, FAR), 128), hot(slots(col, 16, 256), 128)]
+    own = dot(hot(row, EXT), jnp.concatenate(targets, axis=0), NT)
+    for c in range(2):
+        count_v[c] = own[:, c * LANES : (c + 1) * LANES]
+    edge_out[...] = own[:, 256:384]
+
     lane8 = iota((8, LANES), 1)
     lane24 = iota((24, LANES), 1)
     for k, (r, c) in enumerate(CORNERS):
@@ -170,28 +191,8 @@
             upper = pltpu.roll(upper, 64, 1)
         corner_send[k, 8:32, :] = jnp.where(lane24 < 64, upper, lower).astype(I32)
 
-    pl.semaphore_wait(barrier, 8)
-    copies = []
-
-    def send(source, target, step):
-        k = len(copies)
-        copy = pltpu.make_async_remote_copy(
-            source, target, send_sem.at[k], recv_sem.at[k],
-            device_id=device(step), device_id_type=MESH,
-        )
-        copy.start()
-        copies.append(copy)
-
-    send(cells_v, lists_v.at[1], (-1, 0))
-    send(cells_v, lists_v.at[0], (1, 0))
-    send(codes_v.at[pl.ds(0, 32)], s_v, (-1, 0))
-    send(codes_v.at[pl.ds(224, 32)], n_v, (1, 0))
-    send(cells_v, lists_v.at[3], (0, -1))
-    send(cells_v, lists_v.at[2], (0, 1))
     for k, step in enumerate(CORNERS):
         send(corner_send.at[k], corner_out.at[3 - k], step)
-    send(w_send, e_out, (0, -1))
-    send(e_send, w_out, (0, 1))
 
     loads[3].wait()
     block = (row * 1639) >> 16

time: 26.7 us -> 26.7 us (level)
  no operation moved by 1% of the time
where the time goes in v9:
time: 26.7 us; the launch traced here: 26.6 us
  Pallas kernels  25.9 us (97%)
  between operations  0.64 us (2%)
    pallas_call x1, Pallas kernels, exchange(): pl.pallas_call(exchange_kernel, out_shape=(pltpu.VMEM((64, LANES), I32),...  15.9 us
    pallas_call x1, Pallas kernels, frame(): pl.pallas_call(frame_kernel, out_shape=(jax.ShapeDtypeStruct((4, TILE, TI...  10 us

profile of v9, /device:TPU:1, one launch (start us, length us, event | category | flops | bytes accessed | tf_op | source)
XLA Modules:
  0.0 26.6 jit_solution(5172346694314310810)
XLA Ops:
  0.6 15.9 %exchange.1 = (s32[64,128]{1,0:T(8,128)S(1)}, s32[64,128]{1,0:T(8,128)S(1)}, s32[4,32,128]{2,1,0:T(8,128)S(1)}, f32[320,128]{1,0:T(8,128)S(1)}, f32[320,640]{1,0...) custom-call(s32[1,2048]{1,0:T(1,128)} %bitcast.3, ...), custom_call_target="tpu_custom_call" | custom-call | tf_op jit(solution)/shard_map/exchange/pallas_call | solution.py:241
  16.5 10.0 %frame.1 = (f32[4,256,256]{2,1,0:T(8,128)}, f32[1,2048]{1,0:T(1,128)}) custom-call(s32[64,128]{1,0:T(8,128)S(1)} %get-tuple-element.15.w_ref, s32[64,128]{1,0:T(8,128)S(1)} %get-tuple-element.16.e_ref, s32[4,32,128]{2,1,0:T(8,128)S(1)} %get-tuple-element.17.corner_ref, f32[320,128]{1,0:T(8,128)S(1)} %get-tuple-element.18.own_ref, ...), custom_call_target="tpu_custom_call" | custom-call | tf_op jit(solution)/shard_map/frame/pallas_call | solution.py:440
